TPU v7x, 512 devices: a whole 4x8x8 slice. The times are simulated.
512 devices in a mesh: ctx: 64 (over z, y), mp: 8 (over x, core).
Axes of the slice: x: 4, y: 8, z: 8, core: 2. Of those that a mesh axis runs over, the one named last changes fastest.
Arguments:
- seq_in: bfloat16 [8192, 8192], P('ctx', 'mp'), may hold values from -6 to 6
- gate_in: bfloat16 [8192, 8192], P('ctx', 'mp'), may hold values from -6 to 6
- upstream: bfloat16 [8192, 8192], P('ctx', 'mp'), may hold values from -6 to 6
- forget_flags: int32 [8192], P('ctx'), may hold values 0 or 1
- conv_weight: float32 [4, 8192], P(None, 'mp'), may hold values from -3 to 3
- conv_bias: float32 [8192], P('mp'), may hold values from -3 to 3
- proj_weight: bfloat16 [8192, 544], P(('mp', 'ctx')), may hold values from -0.0625 to 0.0625
- dt_weight: bfloat16 [512, 8192], P('ctx', 'mp'), may hold values from -0.25 to 0.25
- dt_bias: float32 [8192], P('mp'), may hold values from -10 to -3
- a_log: float32 [16, 8192], P(None, 'mp'), may hold values from 0 to 2.77
- skip_gain: float32 [8192], P('mp'), may hold values from 0.5 to 1.5
Outputs:
- grad_seq: bfloat16 [8192, 8192], P('ctx', 'mp')
- grad_gate: bfloat16 [8192, 8192], P('ctx', 'mp')
- grad_dt_weight: float32 [512, 8192], P('ctx', 'mp')
- grad_conv_weight: float32 [4, 8192], P(None, ('mp', 'ctx'))
- grad_conv_bias: float32 [8192], P(('mp', 'ctx'))
- grad_dt_bias: float32 [8192], P(('mp', 'ctx'))
- grad_a_log: float32 [16, 8192], P(None, ('mp', 'ctx'))
- grad_skip: float32 [8192], P(('mp', 'ctx'))
All inputs are finite; a program needn't handle non-finite values. No bound on the sum of `forget_flags` on one device may be relied on, other than what follows from the above.
Results may differ from a plain program's by a relative error of at most 0.017.
Values may be sent and summed in bfloat16 or wider, within the bound.
A program may use at most 64 MiB of HBM per device.

v0:
```python
import jax
import jax.numpy as jnp
from jax import lax
from jax.sharding import PartitionSpec as P

STATE = 16
RANK = 512
CONV = 4


def shifted(block, axis, distance):
    devices = range(lax.axis_size(axis))
    route = [(i - distance, i) for i in devices if i - distance in devices]
    return lax.ppermute(block, axis, route)


def prefix(x, axis, combine, identity, reverse):
    count, mine = (lax.axis_size(axis), lax.axis_index(axis))
    everything = jax.tree.map(lambda part: lax.all_gather(part, axis), x)
    start = jax.tree.map(
        lambda part, zero: jnp.broadcast_to(jnp.asarray(zero, part.dtype), part.shape), x, identity
    )

    def step(k, before):
        at = count - 1 - k if reverse else k
        reached = at > mine if reverse else at < mine
        new = combine(before, jax.tree.map(lambda part: part[at], everything))
        return jax.tree.map(lambda a, b: jnp.where(reached, a, b), new, before)

    return lax.fori_loop(0, count, step, start)


def to_blocks(arrays):
    return tuple((a.reshape((a.shape[0] // 16, 16) + a.shape[1:]) for a in arrays))


def block_closed(carry, inputs):
    state, a_matrix = carry
    act_blk, step_blk, b_blk, c_blk = inputs
    rows = step_blk.shape[0]
    cumul = jnp.cumsum(step_blk[:, None, :] * a_matrix[None], axis=0)
    later_rows = lax.broadcasted_iota(jnp.int32, (rows, rows), 0)
    early_rows = lax.broadcasted_iota(jnp.int32, (rows, rows), 1)
    lower = (later_rows >= early_rows)[:, :, None, None]
    gaps = jnp.where(lower, cumul[:, None] - cumul[None, :], 0.0)
    weights = jnp.where(lower, jnp.exp(gaps), 0.0)
    inflow = b_blk[:, :, None] * (step_blk * act_blk)[:, None, :]
    states = jnp.exp(cumul) * state[None] + jnp.sum(weights * inflow[None], axis=1)
    outputs = jnp.sum(c_blk[:, :, None] * states, axis=1)
    return ((states[-1], a_matrix), outputs)


def scan_tokens(act_full, step_size, b_matrix, c_matrix, log_rates, skip):
    a_matrix = -jnp.exp(log_rates)
    length = act_full.shape[0]
    start_state = jnp.zeros(log_rates.shape, jnp.float32)
    carry, outputs = lax.scan(
        jax.checkpoint(block_closed),
        (start_state, a_matrix),
        to_blocks((act_full, step_size, b_matrix, c_matrix)),
    )
    return (outputs.reshape(length, -1) + skip[None, :] * act_full, carry[0])


def carry_block(carry, inputs):
    state, a_matrix = carry
    step_blk, c_blk = inputs
    cumul = jnp.cumsum(step_blk[:, None, :] * a_matrix[None], axis=0)
    states = jnp.exp(cumul) * state[None]
    return ((states[-1], a_matrix), jnp.sum(c_blk[:, :, None] * states, axis=1))


def carry_in(step_size, c_matrix, log_rates, state_in):
    a_matrix = -jnp.exp(log_rates)
    length = step_size.shape[0]
    carry, outputs = lax.scan(
        jax.checkpoint(carry_block), (state_in, a_matrix), to_blocks((step_size, c_matrix))
    )
    return (outputs.reshape(length, -1), carry[0])


def compose(earlier, later):
    return (earlier[0] * later[0], later[0] * earlier[1] + later[1])


def body(
    seq_in,
    gate_in,
    upstream,
    forget_flags,
    conv_weight,
    conv_bias,
    proj_weight,
    dt_weight,
    dt_bias,
    a_log,
    skip_gain,
):
    length = seq_in.shape[0]
    rim_rows = CONV - 1
    from_left = shifted(seq_in[length - rim_rows :], "ctx", 1)
    padded = jnp.concatenate([from_left, seq_in], axis=0)
    pre_act = jnp.zeros(seq_in.shape, jnp.float32) + conv_bias[None, :]
    for k in range(CONV):
        pre_act = pre_act + conv_weight[k][None, :] * padded[k : k + length]
    act_half = jax.nn.silu(pre_act).astype(jnp.bfloat16)
    rows_proj, rows_dt = (
        lax.all_gather(proj_weight, "ctx", axis=0, tiled=True),
        lax.all_gather(dt_weight, "ctx", axis=0, tiled=True),
    )
    partial_proj = jnp.dot(act_half, rows_proj, preferred_element_type=jnp.float32)
    projected = lax.psum(partial_proj, "mp")
    dt_low = projected[:, :RANK].astype(jnp.bfloat16)
    b_matrix = projected[:, RANK : RANK + STATE]
    c_matrix = projected[:, RANK + STATE :]
    dt_pre = jnp.dot(dt_low, rows_dt, preferred_element_type=jnp.float32) + dt_bias[None, :]
    step_size = jax.nn.softplus(dt_pre)
    a_matrix = -jnp.exp(a_log)
    act_full = act_half.astype(jnp.float32)
    (mixed_local, state_end), pull_local = jax.vjp(
        scan_tokens, act_full, step_size, b_matrix, c_matrix, a_log, skip_gain
    )
    zeros_state = jnp.zeros_like(state_end)
    step_totals = jnp.sum(step_size, axis=0)
    decays = jnp.exp(a_matrix * step_totals[None, :])
    state_in = prefix(
        (decays, state_end), "ctx", compose, (jnp.ones_like(decays), zeros_state), False
    )[1]
    (mixed_carry, unused_end), pull_carry = jax.vjp(carry_in, step_size, c_matrix, a_log, state_in)
    mixed = mixed_local + mixed_carry
    flag_values = forget_flags.astype(jnp.float32)
    grad_out = -flag_values[:, None] * upstream.astype(jnp.float32)
    gate_full = gate_in.astype(jnp.float32)
    gate_sigmoid = jax.nn.sigmoid(gate_full)
    grad_mixed = grad_out * (gate_full * gate_sigmoid)
    grad_gate = (
        grad_out * mixed * (gate_sigmoid * (1.0 + gate_full * (1.0 - gate_sigmoid)))
    ).astype(jnp.bfloat16)
    local_adjoint = pull_carry((grad_mixed, zeros_state))[3]
    adjoint_out = prefix(
        (decays, local_adjoint), "ctx", compose, (jnp.ones_like(decays), zeros_state), True
    )[1]
    grad_act_scan, grad_step, grad_bmat, grad_cmat, grad_rate, grad_skip = pull_local(
        (grad_mixed, adjoint_out)
    )
    extra_step, extra_cmat, extra_rate, unused_in = pull_carry((grad_mixed, adjoint_out))
    grad_step = grad_step + extra_step
    grad_cmat = grad_cmat + extra_cmat
    grad_rate = grad_rate + extra_rate
    grad_pre = grad_step * jax.nn.sigmoid(dt_pre)
    grad_pre_half = grad_pre.astype(jnp.bfloat16)
    grad_dtw = lax.dot_general(
        dt_low, grad_pre_half, (((0,), (0,)), ((), ())), preferred_element_type=jnp.float32
    )
    grad_low = lax.dot_general(
        grad_pre_half, rows_dt, (((1,), (1,)), ((), ())), preferred_element_type=jnp.float32
    )
    grad_proj = lax.psum(
        jnp.concatenate([grad_low, grad_bmat, grad_cmat], axis=1).astype(jnp.bfloat16), "mp"
    )
    grad_from_proj = lax.dot_general(
        grad_proj, rows_proj, (((1,), (1,)), ((), ())), preferred_element_type=jnp.float32
    )
    act_sigmoid = jax.nn.sigmoid(pre_act)
    grad_pre_act = (grad_act_scan + grad_from_proj) * (
        act_sigmoid * (1.0 + pre_act * (1.0 - act_sigmoid))
    )
    from_next = shifted(grad_pre_act[:rim_rows], "ctx", -1)
    grad_padded = jnp.concatenate([grad_pre_act, from_next], axis=0)
    grad_seq = jnp.zeros(seq_in.shape, jnp.float32)
    for k in range(CONV):
        grad_seq = (
            grad_seq + conv_weight[k][None, :] * grad_padded[rim_rows - k : rim_rows - k + length]
        )
    grad_conv_w = jnp.stack(
        [jnp.sum(grad_pre_act * padded[k : k + length], axis=0) for k in range(CONV)]
    )
    grad_conv_b = jnp.sum(grad_pre_act, axis=0)
    grad_dt_b = jnp.sum(grad_pre, axis=0)
    summed_grads = (
        lax.psum_scatter(grad_dtw, "ctx", scatter_dimension=0, tiled=True),
        lax.psum_scatter(grad_conv_w, "ctx", scatter_dimension=1, tiled=True),
        lax.psum_scatter(grad_conv_b, "ctx", scatter_dimension=0, tiled=True),
        lax.psum_scatter(grad_dt_b, "ctx", scatter_dimension=0, tiled=True),
        lax.psum_scatter(grad_rate, "ctx", scatter_dimension=1, tiled=True),
        lax.psum_scatter(grad_skip, "ctx", scatter_dimension=0, tiled=True),
    )
    return (grad_seq.astype(jnp.bfloat16), grad_gate) + tuple(summed_grads)


def solution(mesh):
    return jax.shard_map(
        body,
        mesh=mesh,
        in_specs=(
            P("ctx", "mp"),
            P("ctx", "mp"),
            P("ctx", "mp"),
            P("ctx"),
            P(None, "mp"),
            P("mp"),
            P(("mp", "ctx"), None),
            P("ctx", "mp"),
            P("mp"),
            P(None, "mp"),
            P("mp"),
        ),
        out_specs=(
            P("ctx", "mp"),
            P("ctx", "mp"),
            P("ctx", "mp"),
            P(None, ("mp", "ctx")),
            P(("mp", "ctx")),
            P(("mp", "ctx")),
            P(None, ("mp", "ctx")),
            P(("mp", "ctx")),
        ),
        check_vma=False,
    )
```

profile of v0, /device:TPU:6, one launch (start us, length us, event | category | flops | bytes accessed | tf_op | source)
XLA Modules:
  0.0 1251.3 jit_solution(16375797547710604420)
XLA Ops:
  16.4 81.7 %all-gather.9.cloned.1.call-done = bf16[1024,544]{1,0:T(8,128)(2,1)} async-done(((bf16[16,544]{1,0:T(8,128)(2,1)}), bf16[1024,544]{1,0:T(8,128)(2,1)}) %all-gather.9.cloned.1.call-update) | async-done | bytes 1114128 | tf_op jit(solution)/shard_map/all_gather | solution.py:108
  101.8 63.4 %all-reduce.15.cloned.1.call-done = f32[128,544]{0,1:T(8,128)} async-done(((f32[128,544]{0,1:T(8,128)}), f32[128,544]{0,1:T(8,128)}) %all-reduce.15.cloned.1.call-update) | async-done | bytes 278544 | tf_op jit(solution)/shard_map/psum | solution.py:112
  167.4 85.5 %all-gather.11.cloned.1.call-done = bf16[512,1024]{1,0:T(8,128)(2,1)} async-done(((bf16[8,1024]{1,0:T(8,128)(2,1)}), bf16[512,1024]{1,0:T(8,128)(2,1)}) %all-gather.11.cloned.1.call-update) | async-done | bytes 1048592 | tf_op jit(solution)/shard_map/all_gather | solution.py:109
  256.4 59.0 %while.128 = (s32[]{:T(128)}, f32[16,1024]{1,0:T(8,128)S(1)}, f32[8,16,1024]{2,1,0:T(8,128)S(1)}, f32[8,16,1024]{2,1,0:T(8,128)S(1)}, f32[8,16,1024]{2,1,0:T(8,1...) while((s32[]{:T(128)}, f32[16,1024]{1,0:T(8,128)S(1)}, ...), condition=%wide.region_6.7_spmd.clone.clone, body=%wide.region_2.6_spmd.clone.clone.sunk | while | flops 26214400 | bytes 9574793 | solution.py:57
  287.1 5.7 multiply_reduce_fusion.25
  316.7 83.6 %all-gather.15.cloned.1.call-done = f32[1024,1024]{1,0:T(8,128)} async-done(((f32[16,1024]{1,0:T(8,128)}), f32[1024,1024]{1,0:T(8,128)}) %all-gather.15.cloned.1.call-update) | async-done | bytes 4194320 | tf_op jit(solution)/shard_map/all_gather | solution.py:19
  400.3 87.8 %all-gather.13.cloned.1.call-done = f32[1024,1024]{1,0:T(8,128)} async-done(((f32[16,1024]{1,0:T(8,128)}), f32[1024,1024]{1,0:T(8,128)}) %all-gather.13.cloned.1.call-update) | async-done | bytes 4194320 | tf_op jit(solution)/shard_map/all_gather | solution.py:19
  488.1 59.9 %while.129 = (s32[]{:T(128)}, f32[16,1024]{1,0:T(8,128)S(1)}, s32[]{:T(128)}, f32[64,16,1024]{2,1,0:T(8,128)}, f32[64,16,1024]{2,1,0:T(8,128)}, /*index=5*/s32[]{:T(128)}, s32[]{:T(128)}) while((s32[]{:T(128)}, f32[16,1024]{1,0:T(8,128)S(1)}, s32[]{:T(128)}, f32[64,16,1024]{2,1,0:T(8,128)}, f32[64,16,1024]{2,1,0:T(8,128)}, ...), condition=%wide.region_8.9_spmd.clone, body=%wide.region_7.8_spmd.clone.sunk | while | flops 65540 | bytes 262245 | solution.py:30
  549.1 14.5 %while.126 = (s32[]{:T(128)}, f32[16,1024]{1,0:T(8,128)S(1)}, f32[8,16,1024]{2,1,0:T(8,128)S(1)}, f32[8,16,1024]{2,1,0:T(8,128)}, f32[8,16,1024]{2,1,0:T(8,128)S...) while((s32[]{:T(128)}, f32[16,1024]{1,0:T(8,128)S(1)}, ...), condition=%wide.region_12.13_spmd, body=%wide.region_9.12_spmd.sunk | while | flops 4964354 | bytes 1969769 | solution.py:76
  563.6 8.2 while.127
  573.4 83.1 %all-gather.17.cloned.1.call-done = f32[1024,1024]{1,0:T(8,128)} async-done(((f32[16,1024]{1,0:T(8,128)}), f32[1024,1024]{1,0:T(8,128)}) %all-gather.17.cloned.1.call-update) | async-done | bytes 4194320 | tf_op jit(solution)/shard_map/all_gather | solution.py:19
  656.5 60.4 %while.130 = (s32[]{:T(128)}, f32[16,1024]{1,0:T(8,128)S(1)}, s32[]{:T(128)}, f32[64,16,1024]{2,1,0:T(8,128)}, f32[64,16,1024]{2,1,0:T(8,128)}, /*index=5*/s32[]{:T(128)}, s32[]{:T(128)}, s32[]{:T(128)}, s32[]{:T(128)}) while((s32[]{:T(128)}, f32[16,1024]{1,0:T(8,128)S(1)}, s32[]{:T(128)}, f32[64,16,1024]{2,1,0:T(8,128)}, ...), condition=%wide.region_18.19_spmd.clone, body=%wide.region_17.18_spmd.clone.sunk | while | flops 65544 | bytes 262307 | solution.py:30
  716.9 22.7 %while.132 = (s32[]{:T(128)}, f32[16,1024]{1,0:T(8,128)S(1)}, f32[16,1024]{1,0:T(8,128)S(1)}, f32[8,16,1024]{2,1,0:T(8,128)S(1)}, f32[8,16,16]{2,1,0:T(8,128)S(1...) while((s32[]{:T(128)}, f32[16,1024]{1,0:T(8,128)S(1)}, ...), condition=%wide.region_40.41_spmd.clone, body=%wide.region_33.40_spmd.clone.sunk | while | flops 12041988 | bytes 4084903 | solution.py:76
  742.0 138.3 %while.131 = (s32[]{:T(128)}, f32[16,1024]{1,0:T(8,128)S(1)}, f32[16,1024]{1,0:T(8,128)S(1)}, f32[8,16,1024]{2,1,0:T(8,128)}, f32[8,16,1024]{2,1,0:T(8,128)}, /*...) while((s32[]{:T(128)}, f32[16,1024]{1,0:T(8,128)S(1)}, ...), condition=%wide.region_32.33_spmd.clone, body=%wide.region_19.32_spmd.clone.sunk | while | flops 68452096 | bytes 19686096 | solution.py:57
  745.2 10.7 fusion.106
  762.5 10.7 fusion.106
  779.8 10.7 fusion.106
  797.1 10.7 fusion.106
  814.3 10.7 fusion.106
  831.6 10.7 fusion.106
  848.9 10.7 fusion.106
  866.1 10.7 fusion.106
  892.4 57.6 %all-reduce.17.cloned.1.call-done = bf16[128,544]{1,0:T(8,128)(2,1)} async-done(((bf16[128,544]{1,0:T(8,128)(2,1)}), bf16[128,544]{1,0:T(8,128)(2,1)}) %all-reduce.17.cloned.1.call-update) | async-done | bytes 139280 | tf_op jit(solution)/shard_map/psum | solution.py:158
  958.9 280.4 %all-reduce.9 = (f32[4,1024]{1,0:T(4,128)S(1)}, f32[1024]{0:T(1024)S(1)}, f32[1024]{0:T(1024)S(1)}, f32[1024]{0:T(1024)S(1)}) all-reduce(f32[4,1024]{1,0:T(4,128)S(1)} %pad_maximum_fusion.3, f32[1024]{0:T(1024)S(1)} %get-tuple-element.1399, f32[1024]{0:T(1024)S(1)} %copy-done.25, ...), channel_id=6, replica_groups=mesh['ctx'=64,'mp'=8] {'ctx'}, use_global_device_ids=true, to_apply=%region_47.48.clone | all-reduce | flops 7168 | bytes 57344
  (648 shorter events, 315.5 us)
Async XLA Ops:
  7.2 245.7 %copy-start.26 = (f32[1024]{0:T(1024)S(1)}, f32[1024]{0:T(1024)}, u32[]{:S(2)}) copy-start(f32[1024]{0:T(1024)} %param.33) | copy-start | bytes 12292
  7.2 248.4 %copy-start.12 = (f32[16,1024]{1,0:T(8,128)S(1)}, f32[16,1024]{1,0:T(8,128)}, u32[]{:S(2)}) copy-start(f32[16,1024]{1,0:T(8,128)} %param.34) | copy-start | bytes 196612
  7.2 91.0 %all-gather.9.cloned.1.call-start = ((), (), s32[]{:S(2)}) async-start(), calls=%async_computation | async-start | bytes 1331200 | tf_op jit(solution)/shard_map/all_gather | solution.py:108
  7.9 157.3 %all-reduce.15.cloned.1.call-start = ((), (), s32[]{:S(2)}) async-start(), calls=%async_computation.1 | async-start | bytes 557056 | tf_op jit(solution)/shard_map/psum | solution.py:112
  8.7 5.1 collective-permute-start
  13.1 88.6 %copy-start.14 = (f32[1,1024]{1,0:T(1,128)}, f32[1,1024]{1,0:T(1,128)S(1)}, u32[]{:S(2)}) copy-start(f32[1,1024]{1,0:T(1,128)S(1)} %get-tuple-element.1561) | copy-start | bytes 12292
  13.1 88.6 %copy-start.16 = (f32[1,1024]{1,0:T(1,128)}, f32[1,1024]{1,0:T(1,128)S(1)}, u32[]{:S(2)}) copy-start(f32[1,1024]{1,0:T(1,128)S(1)} %get-tuple-element.1562) | copy-start | bytes 12292
  13.1 88.6 %copy-start.18 = (f32[1,1024]{1,0:T(1,128)}, f32[1,1024]{1,0:T(1,128)S(1)}, u32[]{:S(2)}) copy-start(f32[1,1024]{1,0:T(1,128)S(1)} %get-tuple-element.1563) | copy-start | bytes 12292
  13.1 88.6 %copy-start.20 = (f32[1,1024]{1,0:T(1,128)}, f32[1,1024]{1,0:T(1,128)S(1)}, u32[]{:S(2)}) copy-start(f32[1,1024]{1,0:T(1,128)S(1)} %get-tuple-element.1564) | copy-start | bytes 12292
  13.8 241.8 %copy-start.28 = (f32[128]{0:T(128)}, f32[128]{0:T(128)S(1)}, u32[]{:S(2)}) copy-start(f32[128]{0:T(128)S(1)} %convert_negate_fusion.1) | copy-start | bytes 1540
  13.8 87.9 %copy-start.22 = (bf16[3,1024]{1,0:T(4,128)(2,1)}, bf16[3,1024]{1,0:T(4,128)(2,1)S(1)}, u32[]{:S(2)}) copy-start(bf16[3,1024]{1,0:T(4,128)(2,1)S(1)} %collective-permute-done) | copy-start | bytes 18436
  100.9 152.0 %all-gather.11.cloned.1.call-start = ((), (), s32[]{:S(2)}) async-start(), calls=%async_computation.2 | async-start | bytes 1064960 | tf_op jit(solution)/shard_map/all_gather | solution.py:109
  101.6 298.7 %all-gather.15.cloned.1.call-start = ((), (), s32[]{:S(2)}) async-start(), calls=%async_computation.5 | async-start | bytes 4259840 | tf_op jit(solution)/shard_map/all_gather | solution.py:19
  315.4 232.7 %copy-start.7 = (f32[8,16,1024]{2,1,0:T(8,128)}, f32[8,16,1024]{2,1,0:T(8,128)S(1)}, u32[]{:S(2)}) copy-start(f32[8,16,1024]{2,1,0:T(8,128)S(1)} %get-tuple-element.2193) | copy-start | bytes 1572868
  315.4 232.7 %copy-start.8 = (f32[8,16,1024]{2,1,0:T(8,128)}, f32[8,16,1024]{2,1,0:T(8,128)S(1)}, u32[]{:S(2)}) copy-start(f32[8,16,1024]{2,1,0:T(8,128)S(1)} %get-tuple-element.2194) | copy-start | bytes 1572868
  315.4 232.7 %copy-start.4 = (f32[8,16,1024]{2,1,0:T(8,128)}, f32[8,16,1024]{2,1,0:T(8,128)S(1)}, u32[]{:S(2)}) copy-start(f32[8,16,1024]{2,1,0:T(8,128)S(1)} %get-tuple-element.1049) | copy-start | bytes 1572868
  316.0 172.1 %all-gather.13.cloned.1.call-start = ((), (), s32[]{:S(2)}) async-start(), calls=%async_computation.4 | async-start | bytes 4259840 | tf_op jit(solution)/shard_map/all_gather | solution.py:19
  316.6 339.8 %all-gather.17.cloned.1.call-start = ((), (), s32[]{:S(2)}) async-start(), calls=%async_computation.6 | async-start | bytes 4259840 | tf_op jit(solution)/shard_map/all_gather | solution.py:19
  563.6 153.3 %copy-start.5 = (f32[8,16,1024]{2,1,0:T(8,128)}, f32[8,16,1024]{2,1,0:T(8,128)S(1)}, u32[]{:S(2)}) copy-start(f32[8,16,1024]{2,1,0:T(8,128)S(1)} %get-tuple-element.1050) | copy-start | bytes 1572868
  572.5 377.5 %all-reduce.17.cloned.1.call-start = ((), (), s32[]{:S(2)}) async-start(), calls=%async_computation.3 | async-start | bytes 327680 | tf_op jit(solution)/shard_map/psum | solution.py:158
  742.0 142.3 %copy-start.1 = (bf16[512,1024]{1,0:T(8,128)(2,1)S(1)}, bf16[512,1024]{1,0:T(8,128)(2,1)}, u32[]{:S(2)}) copy-start(bf16[512,1024]{1,0:T(8,128)(2,1)} %all-gather.11.cloned.1.call-done) | copy-start | bytes 3145732
  886.4 355.2 %all-reduce.19.cloned.1.call-start = ((), (), s32[]{:S(2)}) async-start(), calls=%async_computation.7 | async-start | bytes 4325376
  892.4 66.5 %copy-start.25 = (f32[1024]{0:T(1024)S(1)}, f32[1024]{0:T(1024)}, u32[]{:S(2)}) copy-start(f32[1024]{0:T(1024)} %get-tuple-element.1529) | copy-start | bytes 12292
  952.0 5.6 collective-permute-start.1
  (15 other events, 585.0 us)
Sparse Core Ops, SparseCore 0:
  11.1 87.0 all-gather.8
  101.0 64.1 all-reduce.14
  168.7 84.1 all-gather.10
  316.2 84.1 all-gather.14
  404.3 83.8 all-gather.12
  572.6 83.8 all-gather.16
  886.5 63.4 all-reduce.16
  953.5 165.4 all-reduce.18
where the time goes:
time: 1260 us; the launch traced here: 1250 us
  waiting for transfers between devices  547 us (43%)
  other arithmetic  308 us (24%)
  blocking collectives  280 us (22%)
  local copies, waits for them, and re-layouts  80.2 us (6%)
  between operations  16 us (1%)
    unnamed x1, blocking collectives  280 us
    all_gather x3, waiting for transfers between devices, prefix(): everything = jax.tree.map(lambda part: lax.all_gather(part, axis), x)  255 us
    select_n x128, other arithmetic, step(): return jax.tree.map(lambda a, b: jnp.where(reached, a, b), new, before)  117 us
    all_gather x1, waiting for transfers between devices, body(): lax.all_gather(dt_weight, 'ctx', axis=0, tiled=True)  85.5 us
    reduce_sum x8, other arithmetic, block_closed(): gaps = jnp.where(lower, cumul[:, None] - cumul[None, :], 0.0)  85.3 us
    all_gather x1, waiting for transfers between devices, body(): lax.all_gather(proj_weight, 'ctx', axis=0, tiled=True)  81.7 us
    psum x1, waiting for transfers between devices, body(): projected = lax.psum(partial_proj, 'mp')  63.4 us
    psum x1, waiting for transfers between devices, body(): lax.psum(jnp.concatenate([grad_low, grad_bmat, grad_cmat], axis=1).astype...  57.6 us
  transfers between devices with their start and end apart: 10, of which 8 were waited for; matrix products, arithmetic and copies ran while one was open for 2% of the time, Pallas kernels for 0%

commit v1 on v0

v1 whole, which is shorter than its diff:
```python
import functools

import jax
import jax.numpy as jnp
from jax import lax
from jax.experimental import pallas as pl
from jax.experimental.pallas import tpu as pltpu
from jax.sharding import PartitionSpec as P

STATE = 16
RANK = 512
CONV = 4
PROJ = RANK + 2 * STATE
LANES = 128
CHUNKS = 8
NY = 8
LOG2E = 1.4426950408889634
MESH = pl.DeviceIdType.MESH
F32, BF16 = jnp.float32, jnp.bfloat16
VMEM = pl.BlockSpec(memory_space=pltpu.VMEM)


def lanes_of(g):
    return pl.ds(pl.multiple_of(g * LANES, LANES), LANES)


def call(kernel, outs, args, scratch=(), collective=None):
    params = dict(vmem_limit_bytes=56 * 1024 * 1024)
    if collective is not None:
        params.update(collective_id=collective, has_side_effects=True)
    return pl.pallas_call(
        kernel,
        out_shape=tuple(jax.ShapeDtypeStruct(s, d) for s, d in outs),
        in_specs=[VMEM] * len(args),
        out_specs=tuple(VMEM for _ in outs),
        scratch_shapes=list(scratch),
        compiler_params=pltpu.CompilerParams(**params),
    )(*args)


def sigmoid(v):
    return 1.0 / (1.0 + jnp.exp(-v))


def where_am_i(ny):
    me = lax.axis_index("ctx")
    return me, lax.div(me, ny), lax.rem(me, ny), lax.axis_index("mp")


def greet(peers):
    barrier = pltpu.get_barrier_semaphore()
    for peer in peers:
        pl.semaphore_signal(barrier, inc=1, device_id=peer, device_id_type=MESH)
    pl.semaphore_wait(barrier, len(peers))


def push(src, dst, send, recv, peer):
    copy = pltpu.make_async_remote_copy(
        src_ref=src, dst_ref=dst, send_sem=send, recv_sem=recv, device_id=peer, device_id_type=MESH
    )
    copy.start()
    return copy


def gather_kernel(nz, ny, n_ctx, w_ref, d_ref, s_ref, wo_ref, do_ref, halo_ref, send, recv):
    me, z, y, m = where_am_i(ny)

    def y_peer(k):
        return (z * ny + lax.rem(y + k + ny, ny), m)

    def z_peer(k):
        return (lax.rem(z + k + nz, nz) * ny + y, m)

    after = (lax.rem(me + 1, n_ctx), m)
    before = (lax.rem(me + n_ctx - 1, n_ctx), m)
    greet(
        [y_peer(k) for k in range(1, ny)] + [z_peer(k) for k in range(1, nz)] + [after, before]
    )
    rows = s_ref.shape[0]
    sent = []

    def go(src, dst, slot, peer):
        copy = push(src, dst, send.at[slot], recv.at[slot], peer)
        sent.append(copy)
        return copy

    halo = go(s_ref.at[pl.ds(rows - 16, 16)], halo_ref, 0, after)
    w_first = [go(w_ref, wo_ref.at[z, y], k, y_peer(k)) for k in range(1, ny)]
    d_first = [go(d_ref, do_ref.at[z, y], 8 + k, z_peer(k)) for k in range(1, nz)]
    wo_ref[z, y] = w_ref[...]
    do_ref[z, y] = d_ref[...]

    def w_hop(k, sign, slot):
        origin = lax.rem(z - sign * (k - 1) + nz, nz)
        return go(wo_ref.at[origin], wo_ref.at[origin], slot, z_peer(sign))

    def d_hop(k, sign, slot):
        origin = lax.rem(y - sign * (k - 1) + ny, ny)
        return go(do_ref.at[:, origin], do_ref.at[:, origin], slot, y_peer(sign))

    w_right = w_left = d_right = d_left = None
    for copy in w_first:
        copy.wait_recv()
    for k in range(1, max(nz, ny) // 2 + 1):
        if w_right is not None:
            w_right.wait_recv()
        w_right = w_hop(k, 1, 16 + k) if k <= nz // 2 else None
        if w_left is not None:
            w_left.wait_recv()
        w_left = w_hop(k, -1, 24 + k) if k <= (nz - 1) // 2 else None
        if k == 1:
            for copy in d_first:
                copy.wait_recv()
        if d_right is not None:
            d_right.wait_recv()
        d_right = d_hop(k, 1, 32 + k) if k <= ny // 2 else None
        if d_left is not None:
            d_left.wait_recv()
        d_left = d_hop(k, -1, 40 + k) if k <= (ny - 1) // 2 else None
    for copy in (w_right, w_left, d_right, d_left):
        if copy is not None:
            copy.wait_recv()
    halo.wait_recv()
    for copy in sent:
        copy.wait_send()


def sum_kernel(n, p_ref, o_ref, r_ref, acc_ref, send, recv):
    me, m = lax.axis_index("ctx"), lax.axis_index("mp")

    def peer(k):
        return (me, lax.rem(m + k, n))

    greet([peer(k) for k in range(1, n)])
    first = [
        push(p_ref.at[lax.rem(m + k, n)], r_ref.at[k], send.at[k], recv.at[k], peer(k))
        for k in range(1, n)
    ]
    total = p_ref[m].astype(F32)
    for k in range(1, n):
        first[k - 1].wait_recv()
        total = total + r_ref[k].astype(F32)
    acc_ref[...] = total.astype(BF16)
    second = [
        push(acc_ref, o_ref.at[m], send.at[n + k], recv.at[n + k], peer(k)) for k in range(1, n)
    ]
    o_ref[m] = acc_ref[...]
    for copy in second:
        copy.wait_recv()
    for copy in first + second:
        copy.wait_send()


def sum_over_mp(part, n, collective):
    tokens = part.shape[0]
    shape = (n, tokens // n, PROJ)
    (out,) = call(
        functools.partial(sum_kernel, n),
        [(shape, BF16)],
        [part.reshape(shape)],
        [
            pltpu.VMEM(shape, BF16),
            pltpu.VMEM(shape[1:], BF16),
            pltpu.SemaphoreType.DMA((2 * n,)),
            pltpu.SemaphoreType.DMA((2 * n,)),
        ],
        collective,
    )
    return out.reshape(tokens, PROJ)


def split_total(total):
    high = total.astype(BF16)
    low = (total - high.astype(F32)).astype(BF16)
    shape = (CHUNKS, LANES)
    return jnp.concatenate(
        [jnp.broadcast_to(high.astype(F32), shape), jnp.broadcast_to(low.astype(F32), shape)], 0
    ).astype(BF16)


def carry_kernel(
    nz, ny, x_ref, alog_ref, o_ref, rx_ref, row_ref, rz_ref, back_ref, fw_ref, bw_ref, send, recv
):
    me, z, y, m = where_am_i(ny)

    def y_peer(k):
        return (z * ny + lax.rem(y + k, ny), m)

    def z_peer(k):
        return (lax.rem(z + k, nz) * ny + y, m)

    greet([y_peer(k) for k in range(1, ny)] + [z_peer(k) for k in range(1, nz)])
    first = [
        push(x_ref.at[lax.rem(y + k, ny)], rx_ref.at[y], send.at[k], recv.at[k], y_peer(k))
        for k in range(1, ny)
    ]
    rx_ref[y] = x_ref[y]
    a2 = -LOG2E * jnp.exp(alog_ref[y])
    for copy in first:
        copy.wait_recv()

    def total_of(block):
        tail = block[2 * STATE :].astype(F32)
        return tail[0:1] + tail[CHUNKS : CHUNKS + 1]

    zero = jnp.zeros((STATE, LANES), F32)
    totals = [total_of(rx_ref[j]) for j in range(ny)]
    forward, sums = zero, jnp.zeros((1, LANES), F32)
    before = []
    for j in range(ny):
        fw_ref[j] = forward
        before.append(sums)
        forward = jnp.exp2(a2 * totals[j]) * forward + rx_ref[j, pl.ds(0, STATE)].astype(F32)
        sums = sums + totals[j]
    backward = zero
    behind = [None] * ny
    tail_sum = jnp.zeros((1, LANES), F32)
    for j in reversed(range(ny)):
        bw_ref[j] = backward
        behind[j] = tail_sum
        backward = jnp.exp2(a2 * totals[j]) * backward + rx_ref[j, pl.ds(STATE, STATE)].astype(F32)
        tail_sum = tail_sum + totals[j]
    row_ref[pl.ds(0, STATE)] = forward.astype(BF16)
    row_ref[pl.ds(STATE, STATE)] = backward.astype(BF16)
    row_ref[pl.ds(2 * STATE, STATE)] = split_total(sums)
    second = [
        push(row_ref, rz_ref.at[z], send.at[8 + k], recv.at[8 + k], z_peer(k))
        for k in range(1, nz)
    ]
    rz_ref[z] = row_ref[...]
    for copy in second:
        copy.wait_recv()
    head, tail = zero, zero
    for k in range(nz):
        block = rz_ref[k]
        fresh = jnp.exp2(a2 * total_of(block)) * head + block[:STATE].astype(F32)
        head = jnp.where(k < z, fresh, head)
    for k in reversed(range(nz)):
        block = rz_ref[k]
        fresh = jnp.exp2(a2 * total_of(block)) * tail + block[STATE : 2 * STATE].astype(F32)
        tail = jnp.where(k > z, fresh, tail)
    for j in range(ny):
        into = fw_ref[j] + jnp.exp2(a2 * before[j]) * head
        outof = bw_ref[j] + jnp.exp2(a2 * behind[j]) * tail
        back_ref[j, pl.ds(0, STATE)] = into.astype(BF16)
        back_ref[j, pl.ds(STATE, STATE)] = outof.astype(BF16)
    third = [
        push(
            back_ref.at[lax.rem(y + k, ny)], o_ref.at[y], send.at[16 + k], recv.at[16 + k], y_peer(k)
        )
        for k in range(1, ny)
    ]
    o_ref[y] = back_ref[y]
    for copy in third:
        copy.wait_recv()
    for copy in first + second + third:
        copy.wait_send()


def scatter_kernel(
    nz,
    ny,
    n_ctx,
    dw_ref,
    sg_ref,
    head_ref,
    dwo_ref,
    sgo_ref,
    halo_ref,
    ra_ref,
    rb_ref,
    sa_ref,
    sb_ref,
    rra_ref,
    rrb_ref,
    sr_ref,
    ss_ref,
    srr_ref,
    send,
    recv,
):
    me, z, y, m = where_am_i(ny)

    def y_of(k):
        return lax.rem(y + k, ny)

    def z_of(k):
        return lax.rem(z + k, nz)

    def y_peer(k):
        return (z * ny + y_of(k), m)

    def z_peer(k):
        return (z_of(k) * ny + y, m)

    after = (lax.rem(me + 1, n_ctx), m)
    before = (lax.rem(me + n_ctx - 1, n_ctx), m)
    greet(
        [y_peer(k) for k in range(1, ny)] + [z_peer(k) for k in range(1, nz)] + [after, before]
    )
    half = dw_ref.shape[3] // 2
    sent = []

    def go(src, dst, slot, peer):
        copy = push(src, dst, send.at[slot], recv.at[slot], peer)
        sent.append(copy)
        return copy

    halo = go(head_ref, halo_ref, 0, before)
    s_first = [go(sg_ref.at[z_of(k)], sr_ref.at[k], k, z_peer(k)) for k in range(1, nz)]
    a_first = [
        go(dw_ref.at[z_of(k), :, :, pl.ds(0, half)], ra_ref.at[k], 8 + k, z_peer(k))
        for k in range(1, nz)
    ]
    b_first = [
        go(dw_ref.at[:, y_of(k), :, pl.ds(half, half)], rb_ref.at[k], 16 + k, y_peer(k))
        for k in range(1, ny)
    ]
    for copy in s_first:
        copy.wait_recv()
    total = sg_ref[z]
    for k in range(1, nz):
        total = total + sr_ref[k]
    ss_ref[...] = total
    s_second = [go(ss_ref, srr_ref.at[k], 24 + k, y_peer(k)) for k in range(1, ny)]
    for copy in a_first:
        copy.wait_recv()

    def add_a(i, carry):
        total = dw_ref[z, i, :, pl.ds(0, half)].astype(F32)
        for k in range(1, nz):
            total = total + ra_ref[k, i].astype(F32)
        sa_ref[i] = total.astype(BF16)
        return carry

    lax.fori_loop(0, ny, add_a, 0)
    a_second = [go(sa_ref.at[y_of(k)], rra_ref.at[k], 32 + k, y_peer(k)) for k in range(1, ny)]
    for copy in b_first:
        copy.wait_recv()

    def add_b(i, carry):
        total = dw_ref[i, y, :, pl.ds(half, half)].astype(F32)
        for k in range(1, ny):
            total = total + rb_ref[k, i].astype(F32)
        sb_ref[i] = total.astype(BF16)
        return carry

    lax.fori_loop(0, nz, add_b, 0)
    b_second = [go(sb_ref.at[z_of(k)], rrb_ref.at[k], 40 + k, z_peer(k)) for k in range(1, nz)]
    for copy in s_second:
        copy.wait_recv()
    total = ss_ref[...]
    for k in range(1, ny):
        total = total + srr_ref[k]
    sgo_ref[...] = total
    for copy in a_second:
        copy.wait_recv()
    total = sa_ref[y].astype(F32)
    for k in range(1, ny):
        total = total + rra_ref[k].astype(F32)
    dwo_ref[:, pl.ds(0, half)] = total
    for copy in b_second:
        copy.wait_recv()
    total = sb_ref[z].astype(F32)
    for k in range(1, nz):
        total = total + rrb_ref[k].astype(F32)
    dwo_ref[:, pl.ds(half, half)] = total
    halo.wait_recv()
    for copy in sent:
        copy.wait_send()


def permutation(tokens, transposed=False):
    row = lax.broadcasted_iota(jnp.int32, (tokens, tokens), 1 if transposed else 0)
    col = lax.broadcasted_iota(jnp.int32, (tokens, tokens), 0 if transposed else 1)
    tics = tokens // CHUNKS
    return jnp.where(col == (row & (CHUNKS - 1)) * tics + (row >> 3), 1.0, 0.0)


def dot(a, b, dims=((1,), (0,))):
    return lax.dot_general(a, b, (dims, ((), ())), preferred_element_type=F32)


def chunk_row():
    return lax.broadcasted_iota(jnp.int32, (1, CHUNKS, LANES), 1)


def with_earlier(x, edge, rim):
    last = pltpu.roll(x[x.shape[0] - rim :], 1, 1)
    last = jnp.where(chunk_row() == 0, edge[edge.shape[0] - rim :][:, None, :], last)
    return jnp.concatenate([last, x], axis=0)


def stacked(value):
    return value.reshape(value.shape[0] // CHUNKS, CHUNKS, LANES)


def flat(value):
    return value.reshape(-1, LANES)


def front_kernel(
    seq_ref,
    halo_ref,
    gate_ref,
    up_ref,
    flag_ref,
    cw_ref,
    cb_ref,
    w_ref,
    act_ref,
    pre_ref,
    g_ref,
    gg_ref,
    x_ref,
    part_ref,
    half_ref,
):
    tokens, width = seq_ref.shape
    first = lax.axis_index("ctx") == 0
    perm = permutation(tokens)
    signed = (perm * -flag_ref[...]).astype(BF16)
    perm = perm.astype(BF16)
    x_ref[...] = dot(perm, seq_ref[...])
    g_ref[...] = dot(perm, gate_ref[...])
    gg_ref[...] = dot(signed, up_ref[...])

    def group(g, carry):
        at = lanes_of(g)
        x = stacked(x_ref[:, at])
        edge = jnp.where(first, 0.0, halo_ref[:, at].astype(F32))
        padded = with_earlier(x, edge, CONV - 1)
        taps = cw_ref[:, at]
        pre = cb_ref[:, at][None] + taps[0:1][None] * padded[: x.shape[0]]
        for k in range(1, CONV):
            pre = pre + taps[k : k + 1][None] * padded[k : k + x.shape[0]]
        pre = flat(pre)
        act = (pre * sigmoid(pre)).astype(BF16)
        pre_ref[:, at] = pre
        half_ref[:, at] = act
        act_ref[:, at] = act.astype(F32)
        gate = g_ref[:, at]
        out = gg_ref[:, at]
        s = sigmoid(gate)
        g_ref[:, at] = out * (gate * s)
        gg_ref[:, at] = out * (s * (1.0 + gate * (1.0 - s)))
        return carry

    lax.fori_loop(0, width // LANES, group, 0)
    part_ref[...] = dot(half_ref[...], w_ref[...]).astype(BF16)


def spread(proj_ref, first, out_ref, tics):
    cols = proj_ref[:, pl.ds(RANK, 2 * STATE)].astype(F32)
    for n in range(STATE):
        col = cols[:, first + n : first + n + 1]
        out_ref[:, n] = stacked(jnp.broadcast_to(col, (tics * CHUNKS, LANES)))


def local_kernel(
    proj_ref,
    dt_ref,
    bias_ref,
    alog_ref,
    act_ref,
    g_ref,
    step_ref,
    sig_ref,
    pe_ref,
    pq_ref,
    x_ref,
    b_ref,
    c_ref,
    low_ref,
):
    tokens, width = act_ref.shape
    tics = tokens // CHUNKS
    pre = dot(proj_ref[:, pl.ds(0, RANK)], dt_ref[...]) + bias_ref[...]
    step_ref[...] = jnp.maximum(pre, 0.0) + jnp.log1p(jnp.exp(-jnp.abs(pre)))
    sig_ref[...] = sigmoid(pre)
    spread(proj_ref, 0, b_ref, tics)
    spread(proj_ref, STATE, c_ref, tics)
    row = chunk_row()

    def group(g, carry):
        at = lanes_of(g)
        a2 = jnp.broadcast_to(
            (-LOG2E * jnp.exp(alog_ref[:, at]))[:, None, :], (STATE, CHUNKS, LANES)
        )

        def ahead(t, carry):
            state, total = carry
            here = pl.ds(pl.multiple_of(t * CHUNKS, CHUNKS), CHUNKS)
            step = step_ref[here, at]
            flow = step * act_ref[here, at]
            state = jnp.exp2(step[None] * a2) * state + b_ref[t] * flow[None]
            return state, total + step

        zero = jnp.zeros((STATE, CHUNKS, LANES), F32)
        state, total = lax.fori_loop(
            0, tics, ahead, (zero, jnp.zeros((CHUNKS, LANES), F32)), unroll=4
        )

        def back(i, adjoint):
            t = tics - 1 - i
            here = pl.ds(pl.multiple_of(t * CHUNKS, CHUNKS), CHUNKS)
            step = step_ref[here, at]
            return jnp.exp2(step[None] * a2) * (c_ref[t] * g_ref[here, at][None] + adjoint)

        adjoint = lax.fori_loop(0, tics, back, zero, unroll=4)
        ones = jnp.exp2(total[None] * a2)
        left, right = ones, ones
        shift = 1
        while shift < CHUNKS:
            in_left = row >= shift
            in_right = row < CHUNKS - shift
            state = state + left * jnp.where(in_left, pltpu.roll(state, shift, 1), 0.0)
            left = left * jnp.where(in_left, pltpu.roll(left, shift, 1), 1.0)
            adjoint = adjoint + right * jnp.where(
                in_right, pltpu.roll(adjoint, CHUNKS - shift, 1), 0.0
            )
            right = right * jnp.where(in_right, pltpu.roll(right, CHUNKS - shift, 1), 1.0)
            shift *= 2
        pe_ref[:, :, at] = state
        pq_ref[:, :, at] = adjoint
        for n in range(STATE):
            low_ref[pl.ds(n, 1)] = state[n, CHUNKS - 1 : CHUNKS]
            low_ref[pl.ds(STATE + n, 1)] = adjoint[n, 0:1]
        x_ref[g, pl.ds(0, 2 * STATE)] = low_ref[...].astype(BF16)
        x_ref[g, pl.ds(2 * STATE, STATE)] = split_total(jnp.sum(total, axis=0, keepdims=True))
        return carry

    lax.fori_loop(0, width // LANES, group, 0)


def main_kernel(
    xin_ref,
    pe_ref,
    pq_ref,
    step_ref,
    sig_ref,
    act_ref,
    g_ref,
    gg_ref,
    proj_ref,
    alog_ref,
    skip_ref,
    dt_ref,
    gate_out,
    gas_ref,
    dw_ref,
    part_ref,
    sg_ref,
    b_ref,
    c_ref,
    h_ref,
    gb_ref,
    gc_ref,
    mix_ref,
    gpre_ref,
):
    tokens, width = act_ref.shape
    tics = tokens // CHUNKS
    spread(proj_ref, 0, b_ref, tics)
    spread(proj_ref, STATE, c_ref, tics)
    row = chunk_row()
    gb_ref[...] = jnp.zeros(gb_ref.shape, F32)
    gc_ref[...] = jnp.zeros(gc_ref.shape, F32)

    def group(g, carry):
        at = lanes_of(g)
        rates = -jnp.exp(alog_ref[:, at])
        shape = (STATE, CHUNKS, LANES)
        a1 = jnp.broadcast_to(rates[:, None, :], shape)
        a2 = a1 * LOG2E
        skip = skip_ref[:, at]
        total = jnp.sum(stacked(step_ref[:, at]), axis=0)[None]
        left, right = total, total
        shift = 1
        while shift < CHUNKS:
            left = left + jnp.where(row >= shift, pltpu.roll(left, shift, 1), 0.0)
            right = right + jnp.where(
                row < CHUNKS - shift, pltpu.roll(right, CHUNKS - shift, 1), 0.0
            )
            shift *= 2
        ends = xin_ref[g].astype(F32)
        into = jnp.broadcast_to(ends[:STATE][:, None, :], shape)
        outof = jnp.broadcast_to(ends[STATE:][:, None, :], shape)
        state = jnp.where(row >= 1, pltpu.roll(pe_ref[:, :, at], 1, 1), 0.0)
        state = state + jnp.exp2(a2 * (left - total)) * into
        adjoint = jnp.where(row < CHUNKS - 1, pltpu.roll(pq_ref[:, :, at], CHUNKS - 1, 1), 0.0)
        adjoint = adjoint + jnp.exp2(a2 * (right - total)) * outof
        h_ref[0] = state

        def ahead(t, state):
            here = pl.ds(pl.multiple_of(t * CHUNKS, CHUNKS), CHUNKS)
            step = step_ref[here, at]
            act = act_ref[here, at]
            state = jnp.exp2(step[None] * a2) * state + b_ref[t] * (step * act)[None]
            h_ref[t + 1] = state
            mixed = jnp.sum(c_ref[t] * state, axis=0) + skip * act
            mix_ref[here, at] = mixed * gg_ref[here, at]
            return state

        lax.fori_loop(0, tics, ahead, state, unroll=2)

        def back(i, carry):
            adjoint, rate_sum, pre_sum, skip_sum = carry
            t = tics - 1 - i
            here = pl.ds(pl.multiple_of(t * CHUNKS, CHUNKS), CHUNKS)
            step = step_ref[here, at]
            act = act_ref[here, at]
            grad = g_ref[here, at]
            lam = c_ref[t] * grad[None] + adjoint
            adjoint = jnp.exp2(step[None] * a2) * lam
            pull = adjoint * h_ref[t]
            gc_ref[t] += h_ref[t + 1] * grad[None]
            gb_ref[t] += lam * (step * act)[None]
            flow = jnp.sum(lam * b_ref[t], axis=0)
            slope = jnp.sum(pull * a1, axis=0)
            gas_ref[here, at] = flow * step + skip * grad
            pre = (flow * act + slope) * sig_ref[here, at]
            gpre_ref[here, at] = pre
            return (adjoint, rate_sum + pull * step[None], pre_sum + pre, skip_sum + grad * act)

        none = jnp.zeros((CHUNKS, LANES), F32)
        _, rate_sum, pre_sum, skip_sum = lax.fori_loop(
            0, tics, back, (adjoint, jnp.zeros(shape, F32), none, none)
        )
        sg_ref[g] = jnp.zeros(sg_ref.shape[1:], F32)
        sg_ref[g, pl.ds(5, 1)] = jnp.sum(pre_sum, axis=0, keepdims=True)
        sg_ref[g, pl.ds(6, 1)] = jnp.sum(skip_sum, axis=0, keepdims=True)
        rate_sum = rate_sum * a1
        for n in range(STATE):
            sg_ref[g, pl.ds(CHUNKS + n, 1)] = jnp.sum(rate_sum[n], axis=0, keepdims=True)
        return carry

    lax.fori_loop(0, width // LANES, group, 0)
    unperm = permutation(tokens, True).astype(BF16)
    gate_out[...] = dot(unperm, mix_ref[...].astype(BF16)).astype(BF16)
    half = gpre_ref[...].astype(BF16)
    low = proj_ref[:, pl.ds(0, RANK)].astype(F32)
    dw_ref[...] = dot(low.T.astype(BF16), half).astype(BF16)
    part_ref[:, pl.ds(0, RANK)] = dot(half, dt_ref[...], ((1,), (1,))).astype(BF16)
    pick = jnp.where(
        lax.broadcasted_iota(jnp.int32, (STATE * LANES, STATE), 0) // LANES
        == lax.broadcasted_iota(jnp.int32, (STATE * LANES, STATE), 1),
        1.0,
        0.0,
    ).astype(BF16)

    def folded(ref):
        side = jnp.concatenate([flat(ref[:, n]) for n in range(STATE)], axis=1)
        return dot(side.astype(BF16), pick)

    part_ref[:, pl.ds(RANK, 2 * STATE)] = jnp.concatenate(
        [folded(gb_ref), folded(gc_ref)], axis=1
    ).astype(BF16)


def tail_kernel(
    proj_ref, w_ref, gas_ref, pre_ref, x_ref, halo_ref, sg_ref, out_ref, sgo_ref, head_ref
):
    tokens, width = gas_ref.shape
    first = lax.axis_index("ctx") == 0
    out_ref[...] = dot(proj_ref[...], w_ref[...], ((1,), (1,)))

    def group(g, carry):
        at = lanes_of(g)
        pre = pre_ref[:, at]
        s = sigmoid(pre)
        grad = (gas_ref[:, at] + out_ref[:, at]) * (s * (1.0 + pre * (1.0 - s)))
        out_ref[:, at] = grad
        grad = stacked(grad)
        edge = jnp.where(first, 0.0, halo_ref[:, at].astype(F32))
        x = stacked(x_ref[:, at])
        padded = with_earlier(x, edge, CONV - 1)
        sgo_ref[g] = sg_ref[g]
        for k in range(CONV):
            part = jnp.sum(grad * padded[k : k + x.shape[0]], axis=0)
            sgo_ref[g, pl.ds(k, 1)] = jnp.sum(part, axis=0, keepdims=True)
        sgo_ref[g, pl.ds(CONV, 1)] = jnp.sum(jnp.sum(grad, axis=0), axis=0, keepdims=True)
        head_ref[:, at] = jnp.zeros((CHUNKS, LANES), F32)
        for k in range(CONV - 1):
            head_ref[pl.ds(k, 1), at] = grad[k, 0:1]
        return carry

    lax.fori_loop(0, width // LANES, group, 0)


def end_kernel(n_ctx, grad_ref, halo_ref, cw_ref, out_ref, sum_ref):
    tokens, width = grad_ref.shape
    last = lax.axis_index("ctx") == n_ctx - 1

    def group(g, carry):
        at = lanes_of(g)
        grad = stacked(grad_ref[:, at])
        edge = jnp.where(last, 0.0, halo_ref[:, at])
        later = pltpu.roll(grad[: CONV - 1], CHUNKS - 1, 1)
        later = jnp.where(chunk_row() == CHUNKS - 1, edge[: CONV - 1][:, None, :], later)
        padded = jnp.concatenate([grad, later], axis=0)
        taps = cw_ref[:, at]
        total = taps[CONV - 1 :][None] * grad
        for k in range(CONV - 1):
            off = CONV - 1 - k
            total = total + taps[k : k + 1][None] * padded[off : off + grad.shape[0]]
        sum_ref[:, at] = flat(total).astype(BF16)
        return carry

    lax.fori_loop(0, width // LANES, group, 0)
    out_ref[...] = dot(permutation(tokens, True).astype(BF16), sum_ref[...]).astype(BF16)


def body(
    ny,
    seq_in,
    gate_in,
    upstream,
    forget_flags,
    conv_weight,
    conv_bias,
    proj_weight,
    dt_weight,
    dt_bias,
    a_log,
    skip_gain,
):
    n_ctx, n_mp = lax.axis_size("ctx"), lax.axis_size("mp")
    nz = n_ctx // ny
    tokens, width = seq_in.shape
    tics = tokens // CHUNKS
    groups = width // LANES
    sems = lambda n: [pltpu.SemaphoreType.DMA((n,)), pltpu.SemaphoreType.DMA((n,))]
    full = (tokens, width)
    w_all, d_all, halo = call(
        functools.partial(gather_kernel, nz, ny, n_ctx),
        [
            ((nz, ny) + proj_weight.shape, BF16),
            ((nz, ny) + dt_weight.shape, BF16),
            ((16, width), BF16),
        ],
        [proj_weight, dt_weight, seq_in],
        sems(48),
        1,
    )
    w_all = w_all.reshape(width, PROJ)
    d_all = d_all.reshape(RANK, width)
    flags = forget_flags.astype(F32).reshape(1, tokens)
    act, pre_act, grad, gate_slope, x, part = call(
        front_kernel,
        [(full, F32)] * 5 + [((tokens, PROJ), BF16)],
        [
            seq_in,
            halo,
            gate_in,
            upstream,
            flags,
            conv_weight,
            conv_bias.reshape(1, width),
            w_all,
        ],
        [pltpu.VMEM(full, BF16)],
    )
    proj = sum_over_mp(part, n_mp, 2)
    wide = (tics, STATE, CHUNKS, LANES)
    step, sig, ends, starts, packed = call(
        local_kernel,
        [
            (full, F32),
            (full, F32),
            ((STATE, CHUNKS, width), F32),
            ((STATE, CHUNKS, width), F32),
            ((groups, 3 * STATE, LANES), BF16),
        ],
        [proj, d_all, dt_bias.reshape(1, width), a_log, act, grad],
        [pltpu.VMEM(wide, F32), pltpu.VMEM(wide, F32), pltpu.VMEM((2 * STATE, LANES), F32)],
    )
    a_blocks = a_log.reshape(STATE, groups, LANES).transpose(1, 0, 2)
    (edges,) = call(
        functools.partial(carry_kernel, nz, ny),
        [((groups, 2 * STATE, LANES), BF16)],
        [packed, a_blocks],
        [
            pltpu.VMEM((ny, 3 * STATE, LANES), BF16),
            pltpu.VMEM((3 * STATE, LANES), BF16),
            pltpu.VMEM((nz, 3 * STATE, LANES), BF16),
            pltpu.VMEM((ny, 2 * STATE, LANES), BF16),
            pltpu.VMEM((ny, STATE, LANES), F32),
            pltpu.VMEM((ny, STATE, LANES), F32),
        ]
        + sems(24),
        3,
    )
    grad_gate, grad_scan, grad_dtw, part, small = call(
        main_kernel,
        [
            (full, BF16),
            (full, F32),
            ((RANK, width), BF16),
            ((tokens, PROJ), BF16),
            ((groups, 24, LANES), F32),
        ],
        [
            edges,
            ends,
            starts,
            step,
            sig,
            act,
            grad,
            gate_slope,
            proj,
            a_log,
            skip_gain.reshape(1, width),
            d_all,
        ],
        [
            pltpu.VMEM(wide, F32),
            pltpu.VMEM(wide, F32),
            pltpu.VMEM((tics + 1,) + wide[1:], F32),
            pltpu.VMEM(wide, F32),
            pltpu.VMEM(wide, F32),
            pltpu.VMEM(full, F32),
            pltpu.VMEM(full, F32),
        ],
    )
    grad_proj = sum_over_mp(part, n_mp, 4)
    grad_pre_act, small, head = call(
        tail_kernel,
        [(full, F32), ((groups, 24, LANES), F32), ((CHUNKS, width), F32)],
        [grad_proj, w_all, grad_scan, pre_act, x, halo, small],
    )
    rows = dt_weight.shape[0]
    half = width // 2
    grad_dtw, small, later = call(
        functools.partial(scatter_kernel, nz, ny, n_ctx),
        [((rows, width), F32), ((24, LANES), F32), ((CHUNKS, width), F32)],
        [grad_dtw.reshape(nz, ny, rows, width), small, head],
        [
            pltpu.VMEM((nz, ny, rows, half), BF16),
            pltpu.VMEM((ny, nz, rows, half), BF16),
            pltpu.VMEM((ny, rows, half), BF16),
            pltpu.VMEM((nz, rows, half), BF16),
            pltpu.VMEM((ny, rows, half), BF16),
            pltpu.VMEM((nz, rows, half), BF16),
            pltpu.VMEM((nz, 24, LANES), F32),
            pltpu.VMEM((24, LANES), F32),
            pltpu.VMEM((ny, 24, LANES), F32),
        ]
        + sems(48),
        5,
    )
    (grad_seq,) = call(
        functools.partial(end_kernel, n_ctx),
        [(full, BF16)],
        [grad_pre_act, later, conv_weight],
        [pltpu.VMEM(full, BF16)],
    )
    share = LANES // ny
    mine = lax.dynamic_slice_in_dim(small, lax.rem(lax.axis_index("ctx"), ny) * share, share, 1)
    return (
        grad_seq,
        grad_gate,
        grad_dtw,
        mine[:CONV],
        mine[CONV],
        mine[5],
        mine[8:],
        mine[6],
    )


def build(mesh, ny):
    return jax.shard_map(
        functools.partial(body, ny),
        mesh=mesh,
        in_specs=(
            P("ctx", "mp"),
            P("ctx", "mp"),
            P("ctx", "mp"),
            P("ctx"),
            P(None, "mp"),
            P("mp"),
            P(("mp", "ctx"), None),
            P("ctx", "mp"),
            P("mp"),
            P(None, "mp"),
            P("mp"),
        ),
        out_specs=(
            P("ctx", "mp"),
            P("ctx", "mp"),
            P("ctx", "mp"),
            P(None, ("mp", "ctx")),
            P(("mp", "ctx")),
            P(("mp", "ctx")),
            P(None, ("mp", "ctx")),
            P(("mp", "ctx")),
        ),
        check_vma=False,
    )


def solution(mesh):
    return build(mesh, NY)
```

time: 1260 us -> 163 us (0.13)
  waiting for transfers between devices: 547 us -> 0 us
  other arithmetic: 308 us -> 1.17 us
  blocking collectives: 280 us -> 0 us
  Pallas kernels: 0 us -> 154 us
  local copies, waits for them, and re-layouts: 80.2 us -> 6.08 us
  between operations: 16 us -> 0.68 us
    all_gather x5 -> x0, waiting for transfers between devices: 422 us -> none  [the longest x3 255 us: prefix(): everything = jax.tree.map(lambda part: lax.all_gather(part, axis), x)]
    unnamed x1 -> x0, blocking collectives: 280 us -> none
    pallas_call x0 -> x10, Pallas kernels: none -> 154 us  [call(): pl.pallas_call(kernel, out_shape=tuple((jax.ShapeDtypeStruct(s, d) for s,...]
    reduce_sum x43 -> x0, other arithmetic: 145 us -> none  [the longest x8 85.3 us: block_closed(): gaps = jnp.where(lower, cumul[:, None] - cumul[None, :], 0.0)]
    psum x2 -> x0, waiting for transfers between devices: 121 us -> none  [the longest x1 63.4 us: body(): projected = lax.psum(partial_proj, 'mp')]
    select_n x128 -> x0, other arithmetic: 117 us -> none  [step(): return jax.tree.map(lambda a, b: jnp.where(reached, a, b), new, before)]
    squeeze x96 -> x1, local copies, waits for them, and re-layouts: 38.2 us -> 1.38 us  [body(): mine[6]]
    another operation x74 -> x0, other arithmetic: 27.4 us -> none  [the longest x32 14.6 us: carry_block(): cumul = jnp.cumsum(step_blk[:, None, :] * a_matrix[None], axis=0)]
  transfers between devices with their start and end apart: 10 -> 0, of which waited for: 8 -> 0; matrix products, arithmetic and copies ran while one was open for 2% -> 0% of each run, Pallas kernels for 0% -> 0%
where the time goes in v1:
time: 163 us; the launch traced here: 162 us
  Pallas kernels  154 us (94%)
  local copies, waits for them, and re-layouts  6.08 us (4%)
    pallas_call x10, Pallas kernels, call(): pl.pallas_call(kernel, out_shape=tuple((jax.ShapeDtypeStruct(s, d) for s,...  154 us

profile of v1, /device:TPU:6, one launch (start us, length us, event | category | flops | bytes accessed | tf_op | source)
XLA Modules:
  0.0 161.6 jit_solution(9206922596117237612)
XLA Ops:
  0.6 44.0 %shard_map.170 = (bf16[8,8,16,544]{3,2,1,0:T(8,128)(2,1)}, bf16[8,8,8,1024]{3,2,1,0:T(8,128)(2,1)}, bf16[16,1024]{1,0:T(8,128)(2,1)}) custom-call(bf16[16,544]{1,0:T(8,128)(2,1)} %w_ref.1, bf16[8,1024]{1,0:T(8,128)(2,1)} %d_ref.1, bf16[128,1024]{1,0:T(8,128)(2,1)} %seq_ref.1), custom_call_target="tpu_custom_call" | custom-call | tf_op jit(solution)/shard_map/pallas_call | solution.py:31
  44.7 1.2 convert_bitcast_fusion.flag_ref
  45.8 4.1 %shard_map.171 = (f32[128,1024]{1,0:T(8,128)}, f32[128,1024]{1,0:T(8,128)}, f32[128,1024]{1,0:T(8,128)}, f32[128,1024]{1,0:T(8,128)}, f32[128,1024]{1,0:T(8,128)}, /*index=5*/bf16[128,544]{1,0:T(8,128)(2,1)}) custom-call(bf16[128,1024]{1,0:T(8,128)(2,1)} %seq_ref.1, bf16[16,1024]{1,0:T(8,128)(2,1)} %get-tuple-element.33.halo_ref, ...), custom_call_target="tpu_custom_call" | custom-call | tf_op jit(solution)/shard_map/pallas_call | solution.py:31
  50.0 0.0 copy-start
  50.0 12.1 %shard_map.172 = bf16[8,16,544]{2,1,0:T(8,128)(2,1)} custom-call(bf16[8,16,544]{2,1,0:T(8,128)(2,1)} %bitcast.34), custom_call_target="tpu_custom_call" | custom-call | tf_op jit(solution)/shard_map/pallas_call | solution.py:31
  62.1 7.8 %shard_map.173 = (f32[128,1024]{1,0:T(8,128)}, f32[128,1024]{1,0:T(8,128)}, f32[16,8,1024]{2,1,0:T(8,128)}, f32[16,8,1024]{2,1,0:T(8,128)}, bf16[8,48,128]{2,1,0:T(8,128)(2,1)}) custom-call(bf16[128,544]{1,0:T(8,128)(2,1)} %bitcast.29, bf16[512,1024]{1,0:T(8,128)(2,1)} %bitcast.27, f32[1,1024]{1,0:T(1,128)} %bitcast.36, f32[16,1024]{1,0:T(8,128)} %alog_ref.3, ...), custom_call_target="tpu_custom_call" | custom-call | tf_op jit(solution)/shard_map/pallas_call | solution.py:31
  69.9 0.0 copy-done
  69.9 0.6 bitcast_bitcast_fusion.alog_ref
  70.6 22.1 %shard_map.174.xin_ref = bf16[8,32,128]{2,1,0:T(8,128)(2,1)} custom-call(bf16[8,48,128]{2,1,0:T(8,128)(2,1)} %get-tuple-element.39.x_ref, f32[8,16,128]{2,1,0:T(8,128)} %bitcast_bitcast_fusion.alog_ref), custom_call_target="tpu_custom_call" | custom-call | tf_op jit(solution)/shard_map/pallas_call | solution.py:31
  92.7 15.3 %shard_map.175 = (bf16[128,1024]{1,0:T(8,128)(2,1)}, f32[128,1024]{1,0:T(8,128)}, bf16[512,1024]{1,0:T(8,128)(2,1)}, bf16[128,544]{1,0:T(8,128)(2,1)}, f32[8,24,128]{2,1,0:T(8,128)}) custom-call(bf16[8,32,128]{2,1,0:T(8,128)(2,1)} %shard_map.174.xin_ref, f32[16,8,1024]{2,1,0:T(8,128)} %get-tuple-element.40.pe_ref, f32[16,8,1024]{2,1,0:T(8,128)} %get-tuple-element.41.pq_ref, ...), custom_call_target="tpu_custom_call" | custom-call | tf_op jit(solution)/shard_map/pallas_call | solution.py:31
  108.0 13.3 %shard_map.176 = bf16[8,16,544]{2,1,0:T(8,128)(2,1)} custom-call(bf16[8,16,544]{2,1,0:T(8,128)(2,1)} %bitcast.33), custom_call_target="tpu_custom_call" | custom-call | tf_op jit(solution)/shard_map/pallas_call | solution.py:31
  121.3 3.7 %shard_map.177 = (f32[128,1024]{1,0:T(8,128)}, f32[8,24,128]{2,1,0:T(8,128)}, f32[8,1024]{1,0:T(8,128)}) custom-call(bf16[128,544]{1,0:T(8,128)(2,1)} %bitcast.32, bf16[1024,544]{1,0:T(8,128)(2,1)} %bitcast.26, f32[128,1024]{1,0:T(8,128)} %get-tuple-element.46.gas_ref, f32[128,1024]{1,0:T(8,128)} %get-tuple-element.47.pre_ref, ...), custom_call_target="tpu_custom_call" | custom-call | tf_op jit(solution)/shard_map/pallas_call | solution.py:31
  125.0 29.0 %shard_map.178 = (f32[8,1024]{1,0:T(8,128)}, f32[24,128]{1,0:T(8,128)}, f32[8,1024]{1,0:T(8,128)}) custom-call(bf16[8,8,8,1024]{3,2,1,0:T(8,128)(2,1)} %bitcast.31, f32[8,24,128]{2,1,0:T(8,128)} %get-tuple-element.52.sg_ref, f32[8,1024]{1,0:T(8,128)} %get-tuple-element.53.head_ref), custom_call_target="tpu_custom_call" | custom-call | tf_op jit(solution)/shard_map/pallas_call | solution.py:31
  154.0 2.2 %shard_map.179 = bf16[128,1024]{1,0:T(8,128)(2,1)} custom-call(f32[128,1024]{1,0:T(8,128)} %get-tuple-element.50.grad_ref, f32[8,1024]{1,0:T(8,128)} %get-tuple-element.54.halo_ref, f32[4,1024]{1,0:T(4,128)} %cw_ref.3), custom_call_target="tpu_custom_call" | custom-call | tf_op jit(solution)/shard_map/pallas_call | solution.py:31
  156.2 1.4 dynamic-slice.3
  157.6 1.4 dynamic-slice_bitcast_fusion
  158.9 1.3 constant_dynamic-slice_fusion
  160.3 1.4 copy.23
Async XLA Ops:
  50.0 20.0 %copy-start = (f32[16,1024]{1,0:T(8,128)S(1)}, f32[16,1024]{1,0:T(8,128)}, u32[]{:S(2)}) copy-start(f32[16,1024]{1,0:T(8,128)} %alog_ref.3) | copy-start | bytes 196612

commit v2 on v0

v2 whole, which is shorter than its diff:
```python
import functools

import jax
import jax.numpy as jnp
from jax import lax
from jax.experimental import pallas as pl
from jax.experimental.pallas import tpu as pltpu
from jax.sharding import PartitionSpec as P

STATE = 16
RANK = 512
CONV = 4
PROJ = RANK + 2 * STATE
LANES = 128
CHUNKS = 8
NY = 8
LOG2E = 1.4426950408889634
MESH = pl.DeviceIdType.MESH
F32, BF16 = jnp.float32, jnp.bfloat16
VMEM = pl.BlockSpec(memory_space=pltpu.VMEM)


def lanes_of(g):
    return pl.ds(pl.multiple_of(g * LANES, LANES), LANES)


def call(kernel, outs, args, scratch=(), collective=None):
    params = dict(vmem_limit_bytes=56 * 1024 * 1024)
    if collective is not None:
        params.update(collective_id=collective, has_side_effects=True)
    return pl.pallas_call(
        kernel,
        out_shape=tuple(jax.ShapeDtypeStruct(s, d) for s, d in outs),
        in_specs=[VMEM] * len(args),
        out_specs=tuple(VMEM for _ in outs),
        scratch_shapes=list(scratch),
        compiler_params=pltpu.CompilerParams(**params),
    )(*args)


def sigmoid(v):
    return 1.0 / (1.0 + jnp.exp(-v))


def split_total(total):
    high = total.astype(BF16)
    low = (total - high.astype(F32)).astype(BF16)
    shape = (CHUNKS, LANES)
    return jnp.concatenate(
        [jnp.broadcast_to(high.astype(F32), shape), jnp.broadcast_to(low.astype(F32), shape)], 0
    ).astype(BF16)


def permutation(tokens, transposed=False):
    row = lax.broadcasted_iota(jnp.int32, (tokens, tokens), 1 if transposed else 0)
    col = lax.broadcasted_iota(jnp.int32, (tokens, tokens), 0 if transposed else 1)
    tics = tokens // CHUNKS
    return jnp.where(col == (row & (CHUNKS - 1)) * tics + (row >> 3), 1.0, 0.0)


def dot(a, b, dims=((1,), (0,))):
    return lax.dot_general(a, b, (dims, ((), ())), preferred_element_type=F32)


def chunk_row():
    return lax.broadcasted_iota(jnp.int32, (1, CHUNKS, LANES), 1)


def with_earlier(x, edge, rim):
    last = pltpu.roll(x[x.shape[0] - rim :], 1, 1)
    last = jnp.where(chunk_row() == 0, edge[edge.shape[0] - rim :][:, None, :], last)
    return jnp.concatenate([last, x], axis=0)


def stacked(value):
    return value.reshape(value.shape[0] // CHUNKS, CHUNKS, LANES)


def flat(value):
    return value.reshape(-1, LANES)


class Net:
    def __init__(self, nz, ny, n_ctx, n_mp, send, recv):
        self.nz, self.ny, self.n_ctx, self.n_mp = nz, ny, n_ctx, n_mp
        self.send, self.recv = send, recv
        self.me, self.m = lax.axis_index("ctx"), lax.axis_index("mp")
        self.z, self.y = lax.div(self.me, ny), lax.rem(self.me, ny)
        self.slots, self.started = 0, []

    def y_of(self, k):
        return lax.rem(self.y + k + self.ny, self.ny)

    def z_of(self, k):
        return lax.rem(self.z + k + self.nz, self.nz)

    def m_of(self, k):
        return lax.rem(self.m + k, self.n_mp)

    def at_y(self, k):
        return (self.z * self.ny + self.y_of(k), self.m)

    def at_z(self, k):
        return (self.z_of(k) * self.ny + self.y, self.m)

    def at_m(self, k):
        return (self.me, self.m_of(k))

    def at_ctx(self, k):
        return (lax.rem(self.me + k + self.n_ctx, self.n_ctx), self.m)

    def greet(self):
        barrier = pltpu.get_barrier_semaphore()
        peers = [self.at_y(k) for k in range(1, self.ny)]
        peers += [self.at_z(k) for k in range(1, self.nz)]
        peers += [self.at_m(k) for k in range(1, self.n_mp)]
        peers += [self.at_ctx(1), self.at_ctx(-1)]
        for peer in peers:
            pl.semaphore_signal(barrier, inc=1, device_id=peer, device_id_type=MESH)
        return lambda: pl.semaphore_wait(barrier, len(peers))

    def take(self, count):
        first = self.slots
        self.slots += count
        return first

    def copy(self, src, dst, slot, peer):
        return pltpu.make_async_remote_copy(
            src_ref=src,
            dst_ref=dst,
            send_sem=self.send.at[slot],
            recv_sem=self.recv.at[slot],
            device_id=peer,
            device_id_type=MESH,
        )

    def go(self, src, dst, peer):
        made = self.copy(src, dst, self.take(1), peer)
        made.start()
        self.started.append(made)
        return made

    def finish(self):
        for made in self.started:
            made.wait_send()


def arrived(copies):
    for made in copies:
        made.wait_recv()


def ring_start(net, size, place, peer, part):
    if size != 8:
        return [net.go(part(place(0), 2), part(place(0), 2), peer(k)) for k in range(1, size)]
    return [net.go(part(place(0), 2), part(place(0), 2), peer(k)) for k in (2, -2, 1, -1)]


def ring_relay(net, size, place, peer, part, first):
    if size != 8:
        arrived(first)
        return []
    arrived(first[:2])
    made = [
        net.go(part(place(-2), 0), part(place(-2), 0), peer(2)),
        net.go(part(place(2), 1), part(place(2), 1), peer(-2)),
        net.go(part(place(-2), 2), part(place(-2), 2), peer(1)),
        net.go(part(place(2), 2), part(place(2), 2), peer(-1)),
    ]
    return made


def cut(ref, size, axis, lanes):
    def part(origin, which):
        span = pl.ds(0, size) if which == 2 else pl.ds(which * (size // 2), size // 2)
        if axis == "z":
            return ref.at[origin, span, :, lanes]
        return ref.at[span, origin, :, lanes]

    return part


def mega_kernel(nz, ny, n_ctx, n_mp, names, *refs):
    r = dict(zip(names, refs))
    net = Net(nz, ny, n_ctx, n_mp, r["send"], r["recv"])
    z, y, m = net.z, net.y, net.m
    seq_ref, alog_ref, skip_ref = r["seq"], r["alog"], r["skip"]
    tokens, width = seq_ref.shape
    tics, groups = tokens // CHUNKS, width // LANES
    half_width = width // 2
    row = chunk_row()
    met = net.greet()

    perm = permutation(tokens)
    signed = (perm * -r["flag"][...].astype(F32)).astype(BF16)
    perm = perm.astype(BF16)
    g_ref, gg_ref, x_ref = r["g"], r["gg"], r["x"]
    x_ref[...] = dot(perm, seq_ref[...])
    g_ref[...] = dot(perm, r["gate"][...])
    gg_ref[...] = dot(signed, r["up"][...])
    wo_ref, do_ref = r["w_all"], r["d_all"]
    wo_ref[z, y] = r["w"][...]
    do_ref[z, y] = r["d"][...]
    met()

    w_cut = 2 * LANES
    w_lo, w_hi = pl.ds(0, w_cut), pl.ds(w_cut, PROJ - w_cut)
    d_lo, d_hi = pl.ds(0, half_width), pl.ds(half_width, half_width)
    halo = net.go(seq_ref.at[pl.ds(tokens - 16, 16)], r["halo"], net.at_ctx(1))

    def first_leg(src, ref, lo, hi):
        a = [net.go(src.at[:, lo], ref.at[z, y, :, lo], net.at_y(k)) for k in range(1, ny)]
        b = [net.go(src.at[:, hi], ref.at[z, y, :, hi], net.at_z(k)) for k in range(1, nz)]
        return a, b

    w_a, w_b = first_leg(r["w"], wo_ref, w_lo, w_hi)
    halo.wait_recv()
    first_block = net.me == 0
    act_ref, pre_ref, actb_ref = r["act"], r["pre"], r["actb"]

    def conv(g, carry):
        at = lanes_of(g)
        x = stacked(x_ref[:, at])
        edge = jnp.where(first_block, 0.0, r["halo"][:, at].astype(F32))
        padded = with_earlier(x, edge, CONV - 1)
        taps = r["cw"][:, at]
        pre = r["cb"][:, at][None] + taps[0:1][None] * padded[: x.shape[0]]
        for k in range(1, CONV):
            pre = pre + taps[k : k + 1][None] * padded[k : k + x.shape[0]]
        pre = flat(pre)
        act = (pre * sigmoid(pre)).astype(BF16)
        pre_ref[:, at] = pre
        actb_ref[:, at] = act
        act_ref[:, at] = act.astype(F32)
        return carry

    lax.fori_loop(0, groups, conv, 0)

    def legs(ref, lo, hi):
        return (
            (nz, net.z_of, net.at_z, cut(ref, ny, "z", lo)),
            (ny, net.y_of, net.at_y, cut(ref, nz, "y", hi)),
        )

    w_za, w_yb = legs(wo_ref, w_lo, w_hi)
    arrived(w_a)
    w_a = ring_start(net, *w_za)
    arrived(w_b)
    w_b = ring_start(net, *w_yb)
    d_a, d_b = first_leg(r["d"], do_ref, d_lo, d_hi)

    def gates(g, carry):
        at = lanes_of(g)
        gate = g_ref[:, at]
        out = gg_ref[:, at]
        s = sigmoid(gate)
        g_ref[:, at] = out * (gate * s)
        gg_ref[:, at] = out * (s * (1.0 + gate * (1.0 - s)))
        return carry

    lax.fori_loop(0, groups, gates, 0)
    w_a2 = ring_relay(net, *w_za, w_a)
    w_b2 = ring_relay(net, *w_yb, w_b)
    d_za, d_yb = legs(do_ref, d_lo, d_hi)
    arrived(d_a)
    d_a = ring_start(net, *d_za)
    arrived(d_b)
    d_b = ring_start(net, *d_yb)
    if nz == 8:
        arrived(w_a[2:])
    if ny == 8:
        arrived(w_b[2:])
    arrived(w_a2 + w_b2)

    sum_shape = (n_mp, tokens // n_mp, PROJ)
    w_full = wo_ref[...].reshape(width, PROJ)
    r["p1"][...] = dot(actb_ref[...], w_full).astype(BF16).reshape(sum_shape)

    def sum_start(p_ref, r_ref):
        return [net.go(p_ref.at[net.m_of(k)], r_ref.at[k], net.at_m(k)) for k in range(1, n_mp)]

    def sum_turn(first, p_ref, r_ref, acc_ref, o_ref):
        total = p_ref[m].astype(F32)
        for k in range(1, n_mp):
            first[k - 1].wait_recv()
            total = total + r_ref[k].astype(F32)
        acc_ref[...] = total.astype(BF16)
        o_ref[m] = acc_ref[...]
        return [net.go(acc_ref, o_ref.at[m], net.at_m(k)) for k in range(1, n_mp)]

    s1 = sum_start(r["p1"], r["q1"])
    d_a2 = ring_relay(net, *d_za, d_a)
    d_b2 = ring_relay(net, *d_yb, d_b)
    s2 = sum_turn(s1, r["p1"], r["q1"], r["acc1"], r["proj"])
    if nz == 8:
        arrived(d_a[2:])
    if ny == 8:
        arrived(d_b[2:])
    arrived(d_a2 + d_b2)

    def lay_out(i, carry):
        rows = do_ref.shape[2] * ny
        block = do_ref[i].astype(F32).reshape(rows, width)
        r["dt"][pl.ds(pl.multiple_of(i * rows, rows), rows)] = block.astype(BF16)
        return carry

    lax.fori_loop(0, nz, lay_out, 0)
    dt_ref = r["dt"]
    arrived(s2)

    proj = r["proj"][...].reshape(tokens, PROJ)
    low = proj[:, :RANK]
    cols = proj[:, RANK:].astype(F32)
    r["low_t"][...] = low.astype(F32).T.astype(BF16)
    step_ref, sig_ref = r["step"], r["sig"]
    step_ref[...] = dot(low, dt_ref[...])
    b_ref, c_ref = r["b"], r["c"]

    def spread(first, out_ref):
        for n in range(STATE):
            col = cols[:, first + n : first + n + 1]
            out_ref[:, n] = stacked(jnp.broadcast_to(col, (tokens, LANES)))

    spread(0, b_ref)
    spread(STATE, c_ref)
    pe_ref, pq_ref, pack_ref, ends_ref = r["pe"], r["pq"], r["pack"], r["ends"]
    wide = (STATE, CHUNKS, LANES)

    def here_of(t):
        return pl.ds(pl.multiple_of(t * CHUNKS, CHUNKS), CHUNKS)

    def local(g, carry):
        at = lanes_of(g)
        pre = step_ref[:, at] + r["dbias"][:, at]
        step_ref[:, at] = jnp.maximum(pre, 0.0) + jnp.log1p(jnp.exp(-jnp.abs(pre)))
        sig_ref[:, at] = sigmoid(pre)
        a2 = jnp.broadcast_to((-LOG2E * jnp.exp(alog_ref[:, at]))[:, None, :], wide)

        def ahead(t, carry):
            state, total = carry
            here = here_of(t)
            step = step_ref[here, at]
            flow = step * act_ref[here, at]
            state = jnp.exp2(step[None] * a2) * state + b_ref[t] * flow[None]
            return state, total + step

        zero = jnp.zeros(wide, F32)
        state, total = lax.fori_loop(
            0, tics, ahead, (zero, jnp.zeros((CHUNKS, LANES), F32)), unroll=4
        )

        def back(i, adjoint):
            t = tics - 1 - i
            here = here_of(t)
            step = step_ref[here, at]
            return jnp.exp2(step[None] * a2) * (c_ref[t] * g_ref[here, at][None] + adjoint)

        adjoint = lax.fori_loop(0, tics, back, zero, unroll=4)
        left = jnp.exp2(total[None] * a2)
        right = left
        shift = 1
        while shift < CHUNKS:
            in_left = row >= shift
            in_right = row < CHUNKS - shift
            state = state + left * jnp.where(in_left, pltpu.roll(state, shift, 1), 0.0)
            left = left * jnp.where(in_left, pltpu.roll(left, shift, 1), 1.0)
            adjoint = adjoint + right * jnp.where(
                in_right, pltpu.roll(adjoint, CHUNKS - shift, 1), 0.0
            )
            right = right * jnp.where(in_right, pltpu.roll(right, CHUNKS - shift, 1), 1.0)
            shift *= 2
        pe_ref[:, :, at] = state
        pq_ref[:, :, at] = adjoint
        for n in range(STATE):
            ends_ref[pl.ds(n, 1)] = state[n, CHUNKS - 1 : CHUNKS]
            ends_ref[pl.ds(STATE + n, 1)] = adjoint[n, 0:1]
        pack_ref[g, pl.ds(0, 2 * STATE)] = ends_ref[...].astype(BF16)
        pack_ref[g, pl.ds(2 * STATE, STATE)] = split_total(jnp.sum(total, axis=0, keepdims=True))
        return carry

    lax.fori_loop(0, groups, local, 0)

    rx_ref, row_ref, rz_ref, back_ref, edge_ref = r["rx"], r["rowt"], r["rz"], r["backt"], r["edges"]
    fw_ref, bw_ref = r["fw"], r["bw"]
    c1 = [net.go(pack_ref.at[net.y_of(k)], rx_ref.at[y], net.at_y(k)) for k in range(1, ny)]
    rx_ref[y] = pack_ref[y]
    my_a2 = -LOG2E * jnp.exp(alog_ref[:, lanes_of(y)])
    gb_ref, gc_ref = r["gb"], r["gc"]
    gb_ref[...] = jnp.zeros(gb_ref.shape, F32)
    gc_ref[...] = jnp.zeros(gc_ref.shape, F32)
    arrived(c1)

    def total_of(block):
        tail = block[2 * STATE :].astype(F32)
        return tail[0:1] + tail[CHUNKS : CHUNKS + 1]

    zero = jnp.zeros((STATE, LANES), F32)
    totals = [total_of(rx_ref[j]) for j in range(ny)]
    forward, sums = zero, jnp.zeros((1, LANES), F32)
    before, behind = [], [None] * ny
    for j in range(ny):
        fw_ref[j] = forward
        before.append(sums)
        forward = jnp.exp2(my_a2 * totals[j]) * forward + rx_ref[j, pl.ds(0, STATE)].astype(F32)
        sums = sums + totals[j]
    backward, tail_sum = zero, jnp.zeros((1, LANES), F32)
    for j in reversed(range(ny)):
        bw_ref[j] = backward
        behind[j] = tail_sum
        backward = jnp.exp2(my_a2 * totals[j]) * backward + rx_ref[j, pl.ds(STATE, STATE)].astype(F32)
        tail_sum = tail_sum + totals[j]
    row_ref[pl.ds(0, STATE)] = forward.astype(BF16)
    row_ref[pl.ds(STATE, STATE)] = backward.astype(BF16)
    row_ref[pl.ds(2 * STATE, STATE)] = split_total(sums)
    c2 = [net.go(row_ref, rz_ref.at[z], net.at_z(k)) for k in range(1, nz)]
    rz_ref[z] = row_ref[...]
    arrived(c2)
    head, tail = zero, zero
    for k in range(nz):
        block = rz_ref[k]
        fresh = jnp.exp2(my_a2 * total_of(block)) * head + block[:STATE].astype(F32)
        head = jnp.where(k < z, fresh, head)
    for k in reversed(range(nz)):
        block = rz_ref[k]
        fresh = jnp.exp2(my_a2 * total_of(block)) * tail + block[STATE : 2 * STATE].astype(F32)
        tail = jnp.where(k > z, fresh, tail)
    for j in range(ny):
        into = fw_ref[j] + jnp.exp2(my_a2 * before[j]) * head
        outof = bw_ref[j] + jnp.exp2(my_a2 * behind[j]) * tail
        back_ref[j, pl.ds(0, STATE)] = into.astype(BF16)
        back_ref[j, pl.ds(STATE, STATE)] = outof.astype(BF16)
    c3 = [net.go(back_ref.at[net.y_of(k)], edge_ref.at[y], net.at_y(k)) for k in range(1, ny)]
    edge_ref[y] = back_ref[y]
    arrived(c3)

    h_ref, mix_ref, gpre_ref, half_ref = r["h"], r["mix"], r["gpre"], r["half"]
    gas_ref, dw_ref, ra_ref, sg_ref = r["gas"], r["dw"], r["ra"], r["sg"]
    base = net.take(groups * 8)

    def dw_copy(g, k, along_z):
        at = lanes_of(g)
        if along_z:
            src, peer = dw_ref.at[net.z_of(k), :, :, at], net.at_z(k)
        else:
            src, peer = dw_ref.at[:, net.y_of(k), :, at], net.at_y(k)
        return net.copy(src, ra_ref.at[k, :, :, at], base + g * 8 + k, peer)

    def main(i, carry):
        g = lax.rem(i, 2) * (groups // 2) + lax.div(i, 2)
        at = lanes_of(g)
        rates = -jnp.exp(alog_ref[:, at])
        a1 = jnp.broadcast_to(rates[:, None, :], wide)
        a2 = a1 * LOG2E
        skip = skip_ref[:, at]
        total = jnp.sum(stacked(step_ref[:, at]), axis=0)[None]
        left, right = total, total
        shift = 1
        while shift < CHUNKS:
            left = left + jnp.where(row >= shift, pltpu.roll(left, shift, 1), 0.0)
            right = right + jnp.where(
                row < CHUNKS - shift, pltpu.roll(right, CHUNKS - shift, 1), 0.0
            )
            shift *= 2
        ends = edge_ref[g].astype(F32)
        into = jnp.broadcast_to(ends[:STATE][:, None, :], wide)
        outof = jnp.broadcast_to(ends[STATE:][:, None, :], wide)
        state = jnp.where(row >= 1, pltpu.roll(pe_ref[:, :, at], 1, 1), 0.0)
        state = state + jnp.exp2(a2 * (left - total)) * into
        adjoint = jnp.where(row < CHUNKS - 1, pltpu.roll(pq_ref[:, :, at], CHUNKS - 1, 1), 0.0)
        adjoint = adjoint + jnp.exp2(a2 * (right - total)) * outof
        h_ref[0] = state

        def ahead(t, state):
            here = here_of(t)
            step = step_ref[here, at]
            act = act_ref[here, at]
            state = jnp.exp2(step[None] * a2) * state + b_ref[t] * (step * act)[None]
            h_ref[t + 1] = state
            mixed = jnp.sum(c_ref[t] * state, axis=0) + skip * act
            mix_ref[here] = mixed * gg_ref[here, at]
            return state

        lax.fori_loop(0, tics, ahead, state, unroll=2)
        r["mixo"][:, at] = mix_ref[...].astype(BF16)

        def back(i, carry):
            adjoint, rate_sum, pre_sum, skip_sum = carry
            t = tics - 1 - i
            here = here_of(t)
            step = step_ref[here, at]
            act = act_ref[here, at]
            grad = g_ref[here, at]
            lam = c_ref[t] * grad[None] + adjoint
            adjoint = jnp.exp2(step[None] * a2) * lam
            pull = adjoint * h_ref[t]
            gc_ref[t] += h_ref[t + 1] * grad[None]
            gb_ref[t] += lam * (step * act)[None]
            flow = jnp.sum(lam * b_ref[t], axis=0)
            slope = jnp.sum(pull * a1, axis=0)
            gas_ref[here, at] = flow * step + skip * grad
            pre = (flow * act + slope) * sig_ref[here, at]
            gpre_ref[here] = pre
            return (adjoint, rate_sum + pull * step[None], pre_sum + pre, skip_sum + grad * act)

        none = jnp.zeros((CHUNKS, LANES), F32)
        _, rate_sum, pre_sum, skip_sum = lax.fori_loop(
            0, tics, back, (adjoint, jnp.zeros(wide, F32), none, none)
        )
        half = gpre_ref[...].astype(BF16)
        half_ref[:, at] = half
        dw_ref[:, :, :, at] = (
            dot(r["low_t"][...], half).reshape(dw_ref.shape[:3] + (LANES,)).astype(BF16)
        )

        @pl.when(g < groups // 2)
        def _():
            for k in range(1, nz):
                dw_copy(g, k, True).start()

        @pl.when(g >= groups // 2)
        def _():
            for k in range(1, ny):
                dw_copy(g, k, False).start()

        sg_ref[g] = jnp.zeros(sg_ref.shape[1:], F32)
        sg_ref[g, pl.ds(5, 1)] = jnp.sum(pre_sum, axis=0, keepdims=True)
        sg_ref[g, pl.ds(6, 1)] = jnp.sum(skip_sum, axis=0, keepdims=True)
        rate_sum = rate_sum * a1
        for n in range(STATE):
            sg_ref[g, pl.ds(CHUNKS + n, 1)] = jnp.sum(rate_sum[n], axis=0, keepdims=True)
        return carry

    lax.fori_loop(0, groups, main, 0)

    pick = jnp.where(
        lax.broadcasted_iota(jnp.int32, (STATE * LANES, STATE), 0) // LANES
        == lax.broadcasted_iota(jnp.int32, (STATE * LANES, STATE), 1),
        1.0,
        0.0,
    ).astype(BF16)

    def folded(ref):
        side = jnp.concatenate([flat(ref[:, n]) for n in range(STATE)], axis=1)
        return dot(side.astype(BF16), pick)

    r["p2"][:, :, pl.ds(0, RANK)] = (
        dot(half_ref[...], dt_ref[...], ((1,), (1,))).astype(BF16).reshape(sum_shape[:2] + (RANK,))
    )
    r["p2"][:, :, pl.ds(RANK, 2 * STATE)] = (
        jnp.concatenate([folded(gb_ref), folded(gc_ref)], axis=1)
        .astype(BF16)
        .reshape(sum_shape[:2] + (2 * STATE,))
    )
    s3 = sum_start(r["p2"], r["q2"])
    sa_ref, sb_ref, rra_ref, rrb_ref = r["sa"], r["sb"], r["rra"], r["rrb"]
    lo, hi = pl.ds(0, half_width), pl.ds(half_width, half_width)
    half_groups = groups // 2

    def add_a(i, carry):
        total = dw_ref[z, i, :, lo].astype(F32)
        for k in range(1, nz):
            total = total + ra_ref[k, i, :, lo].astype(F32)
        sa_ref[i] = total.astype(BF16)
        return carry

    def add_b(i, carry):
        total = dw_ref[i, y, :, hi].astype(F32)
        for k in range(1, ny):
            total = total + ra_ref[k, i, :, hi].astype(F32)
        sb_ref[i] = total.astype(BF16)
        return carry

    s4 = sum_turn(s3, r["p2"], r["q2"], r["acc2"], r["gproj"])
    arrived([dw_copy(g, k, True) for g in range(half_groups) for k in range(1, nz)])
    lax.fori_loop(0, ny, add_a, 0)
    a2nd = [net.go(sa_ref.at[net.y_of(k)], rra_ref.at[k], net.at_y(k)) for k in range(1, ny)]
    arrived([dw_copy(g, k, False) for g in range(half_groups, groups) for k in range(1, ny)])
    lax.fori_loop(0, nz, add_b, 0)
    b2nd = [net.go(sb_ref.at[net.z_of(k)], rrb_ref.at[k], net.at_z(k)) for k in range(1, nz)]
    arrived(s4)

    out_ref, head_ref = r["grad"], r["head"]
    out_ref[...] = dot(r["gproj"][...].reshape(tokens, PROJ), wo_ref[...].reshape(width, PROJ), ((1,), (1,)))

    def close(g, carry):
        at = lanes_of(g)
        pre = pre_ref[:, at]
        s = sigmoid(pre)
        grad = (gas_ref[:, at] + out_ref[:, at]) * (s * (1.0 + pre * (1.0 - s)))
        out_ref[:, at] = grad
        grad = stacked(grad)
        edge = jnp.where(first_block, 0.0, r["halo"][:, at].astype(F32))
        x = stacked(x_ref[:, at])
        padded = with_earlier(x, edge, CONV - 1)
        for k in range(CONV):
            part = jnp.sum(grad * padded[k : k + x.shape[0]], axis=0)
            sg_ref[g, pl.ds(k, 1)] = jnp.sum(part, axis=0, keepdims=True)
        sg_ref[g, pl.ds(CONV, 1)] = jnp.sum(jnp.sum(grad, axis=0), axis=0, keepdims=True)
        head_ref[:, at] = jnp.zeros((CHUNKS, LANES), F32)
        for k in range(CONV - 1):
            head_ref[pl.ds(k, 1), at] = grad[k, 0:1]
        return carry

    lax.fori_loop(0, groups, close, 0)
    t1 = [net.go(sg_ref.at[net.z_of(k)], r["sr"].at[k], net.at_z(k)) for k in range(1, nz)]
    later = net.go(head_ref, r["later"], net.at_ctx(-1))
    arrived(a2nd)
    total = sa_ref[y].astype(F32)
    for k in range(1, ny):
        total = total + rra_ref[k].astype(F32)
    r["dwo"][:, lo] = total
    arrived(b2nd)
    total = sb_ref[z].astype(F32)
    for k in range(1, nz):
        total = total + rrb_ref[k].astype(F32)
    r["dwo"][:, hi] = total
    arrived(t1)
    total = sg_ref[z]
    for k in range(1, nz):
        total = total + r["sr"][k]
    r["ss"][...] = total
    t2 = [net.go(r["ss"], r["srr"].at[k], net.at_y(k)) for k in range(1, ny)]
    later.wait_recv()
    arrived(t2)
    total = r["ss"][...]
    for k in range(1, ny):
        total = total + r["srr"][k]
    r["smallo"][...] = total
    for g in range(groups):
        along_z = g < half_groups
        for k in range(1, nz if along_z else ny):
            dw_copy(g, k, along_z).wait_send()
    net.finish()


def end_kernel(
    n_ctx,
    ny,
    grad_ref,
    halo_ref,
    cw_ref,
    mix_ref,
    dwo_ref,
    small_ref,
    out_ref,
    gate_ref,
    dw_ref,
    w_ref,
    b_ref,
    t_ref,
    a_ref,
    s_ref,
    sum_ref,
):
    tokens, width = grad_ref.shape
    me = lax.axis_index("ctx")
    last = me == n_ctx - 1

    def group(g, carry):
        at = lanes_of(g)
        grad = stacked(grad_ref[:, at])
        edge = jnp.where(last, 0.0, halo_ref[:, at])
        later = pltpu.roll(grad[: CONV - 1], CHUNKS - 1, 1)
        later = jnp.where(chunk_row() == CHUNKS - 1, edge[: CONV - 1][:, None, :], later)
        padded = jnp.concatenate([grad, later], axis=0)
        taps = cw_ref[:, at]
        total = taps[CONV - 1 :][None] * grad
        for k in range(CONV - 1):
            off = CONV - 1 - k
            total = total + taps[k : k + 1][None] * padded[off : off + grad.shape[0]]
        sum_ref[:, at] = flat(total).astype(BF16)
        return carry

    lax.fori_loop(0, width // LANES, group, 0)
    unperm = permutation(tokens, True).astype(BF16)
    out_ref[...] = dot(unperm, sum_ref[...]).astype(BF16)
    gate_ref[...] = dot(unperm, mix_ref[...]).astype(BF16)
    dw_ref[...] = dwo_ref[...]
    share = LANES // ny
    mine = small_ref[...]
    shift = lax.rem(LANES - lax.rem(me, ny) * share, LANES)
    mine = pltpu.roll(mine, shift, 1)[:, :share]
    w_ref[...] = mine[:CONV]
    b_ref[...] = mine[CONV : CONV + 1]
    t_ref[...] = mine[5:6]
    s_ref[...] = mine[6:7]
    a_ref[...] = mine[CHUNKS:]


def body(
    ny,
    seq_in,
    gate_in,
    upstream,
    forget_flags,
    conv_weight,
    conv_bias,
    proj_weight,
    dt_weight,
    dt_bias,
    a_log,
    skip_gain,
):
    n_ctx, n_mp = lax.axis_size("ctx"), lax.axis_size("mp")
    nz = n_ctx // ny
    tokens, width = seq_in.shape
    tics, groups = tokens // CHUNKS, width // LANES
    rows, half, most = dt_weight.shape[0], width // 2, max(nz, ny)
    full, wide = (tokens, width), (tics, STATE, CHUNKS, LANES)
    line = (1, width)
    inputs = dict(
        seq=seq_in,
        gate=gate_in,
        up=upstream,
        flag=forget_flags.reshape(1, tokens),
        cw=conv_weight,
        cb=conv_bias.reshape(line),
        w=proj_weight,
        d=dt_weight,
        dbias=dt_bias.reshape(line),
        alog=a_log,
        skip=skip_gain.reshape(line),
    )
    outs = dict(
        grad=(full, F32),
        later=((CHUNKS, width), F32),
        mixo=(full, BF16),
        dwo=((rows, width), F32),
        smallo=((24, LANES), F32),
    )
    part = (n_mp, tokens // n_mp, PROJ)
    scratch = dict(
        x=(full, F32),
        g=(full, F32),
        gg=(full, F32),
        act=(full, F32),
        pre=(full, F32),
        step=(full, F32),
        sig=(full, F32),
        gas=(full, F32),
        actb=(full, BF16),
        half=(full, BF16),
        halo=((16, width), BF16),
        w_all=((nz, ny) + proj_weight.shape, BF16),
        d_all=((nz, ny) + dt_weight.shape, BF16),
        dt=((RANK, width), BF16),
        low_t=((RANK, tokens), BF16),
        p1=(part, BF16),
        q1=(part, BF16),
        acc1=(part[1:], BF16),
        proj=(part, BF16),
        p2=(part, BF16),
        q2=(part, BF16),
        acc2=(part[1:], BF16),
        gproj=(part, BF16),
        b=(wide, F32),
        c=(wide, F32),
        gb=(wide, F32),
        gc=(wide, F32),
        h=((tics + 1,) + wide[1:], F32),
        pe=((STATE, CHUNKS, width), F32),
        pq=((STATE, CHUNKS, width), F32),
        pack=((groups, 3 * STATE, LANES), BF16),
        ends=((2 * STATE, LANES), F32),
        rx=((ny, 3 * STATE, LANES), BF16),
        rowt=((3 * STATE, LANES), BF16),
        rz=((nz, 3 * STATE, LANES), BF16),
        backt=((ny, 2 * STATE, LANES), BF16),
        edges=((groups, 2 * STATE, LANES), BF16),
        fw=((ny, STATE, LANES), F32),
        bw=((ny, STATE, LANES), F32),
        mix=((tokens, LANES), F32),
        gpre=((tokens, LANES), F32),
        dw=((nz, ny, rows, width), BF16),
        ra=((most, most, rows, width), BF16),
        sa=((ny, rows, half), BF16),
        sb=((nz, rows, half), BF16),
        rra=((ny, rows, half), BF16),
        rrb=((nz, rows, half), BF16),
        sg=((groups, 24, LANES), F32),
        sr=((nz, 24, LANES), F32),
        ss=((24, LANES), F32),
        srr=((ny, 24, LANES), F32),
        head=((CHUNKS, width), F32),
    )
    names = list(inputs) + list(outs) + list(scratch) + ["send", "recv"]
    slots = 256
    grad, later, mix, dwo, small = call(
        functools.partial(mega_kernel, nz, ny, n_ctx, n_mp, names),
        list(outs.values()),
        list(inputs.values()),
        [pltpu.VMEM(s, d) for s, d in scratch.values()]
        + [pltpu.SemaphoreType.DMA((slots,)), pltpu.SemaphoreType.DMA((slots,))],
        1,
    )
    share = LANES // ny
    grad_seq, grad_gate, grad_dtw, g_w, g_b, g_t, g_a, g_s = call(
        functools.partial(end_kernel, n_ctx, ny),
        [
            (full, BF16),
            (full, BF16),
            ((rows, width), F32),
            ((CONV, share), F32),
            ((1, share), F32),
            ((1, share), F32),
            ((STATE, share), F32),
            ((1, share), F32),
        ],
        [grad, later, conv_weight, mix, dwo, small],
        [pltpu.VMEM(full, BF16)],
    )
    return (
        grad_seq,
        grad_gate,
        grad_dtw,
        g_w,
        g_b.reshape(share),
        g_t.reshape(share),
        g_a,
        g_s.reshape(share),
    )


def build(mesh, ny):
    return jax.shard_map(
        functools.partial(body, ny),
        mesh=mesh,
        in_specs=(
            P("ctx", "mp"),
            P("ctx", "mp"),
            P("ctx", "mp"),
            P("ctx"),
            P(None, "mp"),
            P("mp"),
            P(("mp", "ctx"), None),
            P("ctx", "mp"),
            P("mp"),
            P(None, "mp"),
            P("mp"),
        ),
        out_specs=(
            P("ctx", "mp"),
            P("ctx", "mp"),
            P("ctx", "mp"),
            P(None, ("mp", "ctx")),
            P(("mp", "ctx")),
            P(("mp", "ctx")),
            P(None, ("mp", "ctx")),
            P(("mp", "ctx")),
        ),
        check_vma=False,
    )


def solution(mesh):
    return build(mesh, NY)
```

time: 1260 us -> 108 us (0.09)
  waiting for transfers between devices: 547 us -> 0 us
  other arithmetic: 308 us -> 0 us
  blocking collectives: 280 us -> 0 us
  Pallas kernels: 0 us -> 106 us
  local copies, waits for them, and re-layouts: 80.2 us -> 0 us
  between operations: 16 us -> 0.64 us
    all_gather x5 -> x0, waiting for transfers between devices: 422 us -> none  [the longest x3 255 us: prefix(): everything = jax.tree.map(lambda part: lax.all_gather(part, axis), x)]
    unnamed x1 -> x0, blocking collectives: 280 us -> none
    reduce_sum x43 -> x0, other arithmetic: 145 us -> none  [the longest x8 85.3 us: block_closed(): gaps = jnp.where(lower, cumul[:, None] - cumul[None, :], 0.0)]
    psum x2 -> x0, waiting for transfers between devices: 121 us -> none  [the longest x1 63.4 us: body(): projected = lax.psum(partial_proj, 'mp')]
    select_n x128 -> x0, other arithmetic: 117 us -> none  [step(): return jax.tree.map(lambda a, b: jnp.where(reached, a, b), new, before)]
    pallas_call x0 -> x2, Pallas kernels: none -> 106 us  [call(): pl.pallas_call(kernel, out_shape=tuple((jax.ShapeDtypeStruct(s, d) for s,...]
    squeeze x96 -> x0, local copies, waits for them, and re-layouts: 38.2 us -> none  [the longest x80 38.1 us: scan_tokens(): lax.scan(jax.checkpoint(block_closed), (start_state, a_matrix), to_blocks...]
    another operation x74 -> x0, other arithmetic: 27.4 us -> none  [the longest x32 14.6 us: carry_block(): cumul = jnp.cumsum(step_blk[:, None, :] * a_matrix[None], axis=0)]
  transfers between devices with their start and end apart: 10 -> 0, of which waited for: 8 -> 0; matrix products, arithmetic and copies ran while one was open for 2% -> 0% of each run, Pallas kernels for 0% -> 0%
where the time goes in v2:
time: 108 us; the launch traced here: 106 us
  Pallas kernels  106 us (98%)
    pallas_call x2, Pallas kernels, call(): pl.pallas_call(kernel, out_shape=tuple((jax.ShapeDtypeStruct(s, d) for s,...  106 us

profile of v2, /device:TPU:6, one launch (start us, length us, event | category | flops | bytes accessed | tf_op | source)
XLA Modules:
  0.0 106.5 jit_solution(15955354638636456851)
XLA Ops:
  0.6 103.4 %shard_map.170 = (f32[128,1024]{1,0:T(8,128)}, f32[8,1024]{1,0:T(8,128)}, bf16[128,1024]{1,0:T(8,128)(2,1)}, f32[8,1024]{1,0:T(8,128)}, f32[24,128]{1,0:T(8,128)}) custom-call(bf16[128,1024]{1,0:T(8,128)(2,1)} %refs_0_.1, bf16[128,1024]{1,0:T(8,128)(2,1)} %refs_1_.1, bf16[128,1024]{1,0:T(8,128)(2,1)} %refs_2_.1, s32[1,128]{1,0:T(1,128)} %bitcast.10, ...), custom_call_target="tpu_custom_call" | custom-call | tf_op jit(solution)/shard_map/pallas_call | solution.py:31
  104.1 2.4 %shard_map.171 = (bf16[128,1024]{1,0:T(8,128)(2,1)}, bf16[128,1024]{1,0:T(8,128)(2,1)}, f32[8,1024]{1,0:T(8,128)}, f32[4,16]{1,0:T(4,128)}, f32[1,16]{1,0:T(1,12...) custom-call(f32[128,1024]{1,0:T(8,128)} %get-tuple-element.21.grad_ref, ...), custom_call_target="tpu_custom_call" | custom-call | tf_op jit(solution)/shard_map/pallas_call | solution.py:31

commit v3 on v2

--- a/solution.py
+++ b/solution.py
@@ -15,6 +15,10 @@
 CHUNKS = 8
 NY = 8
 LOG2E = 1.4426950408889634
+LN2 = 0.6931471805599453
+SPLIT = 2
+UNROLL_F = 2
+UNROLL_B = 2
 MESH = pl.DeviceIdType.MESH
 F32, BF16 = jnp.float32, jnp.bfloat16
 VMEM = pl.BlockSpec(memory_space=pltpu.VMEM)
@@ -189,24 +193,13 @@
     tics, groups = tokens // CHUNKS, width // LANES
     half_width = width // 2
     row = chunk_row()
-    met = net.greet()
-
-    perm = permutation(tokens)
-    signed = (perm * -r["flag"][...].astype(F32)).astype(BF16)
-    perm = perm.astype(BF16)
     g_ref, gg_ref, x_ref = r["g"], r["gg"], r["x"]
-    x_ref[...] = dot(perm, seq_ref[...])
-    g_ref[...] = dot(perm, r["gate"][...])
-    gg_ref[...] = dot(signed, r["up"][...])
     wo_ref, do_ref = r["w_all"], r["d_all"]
-    wo_ref[z, y] = r["w"][...]
-    do_ref[z, y] = r["d"][...]
-    met()
+    net.greet()()
 
     w_cut = 2 * LANES
     w_lo, w_hi = pl.ds(0, w_cut), pl.ds(w_cut, PROJ - w_cut)
     d_lo, d_hi = pl.ds(0, half_width), pl.ds(half_width, half_width)
-    halo = net.go(seq_ref.at[pl.ds(tokens - 16, 16)], r["halo"], net.at_ctx(1))
 
     def first_leg(src, ref, lo, hi):
         a = [net.go(src.at[:, lo], ref.at[z, y, :, lo], net.at_y(k)) for k in range(1, ny)]
@@ -214,6 +207,27 @@
         return a, b
 
     w_a, w_b = first_leg(r["w"], wo_ref, w_lo, w_hi)
+    halo = net.go(seq_ref.at[pl.ds(tokens - 16, 16)], r["halo"], net.at_ctx(1))
+    perm = permutation(tokens)
+    signed = (perm * -r["flag"][...].astype(F32)).astype(BF16)
+    perm = perm.astype(BF16)
+    x_ref[...] = dot(perm, seq_ref[...])
+    g_ref[...] = dot(perm, r["gate"][...])
+    gg_ref[...] = dot(signed, r["up"][...])
+    wo_ref[z, y] = r["w"][...]
+    do_ref[z, y] = r["d"][...]
+    def legs(ref, lo, hi):
+        return (
+            (nz, net.z_of, net.at_z, cut(ref, ny, "z", lo)),
+            (ny, net.y_of, net.at_y, cut(ref, nz, "y", hi)),
+        )
+
+    w_za, w_yb = legs(wo_ref, w_lo, w_hi)
+    arrived(w_a)
+    w_a = ring_start(net, *w_za)
+    arrived(w_b)
+    w_b = ring_start(net, *w_yb)
+    d_a, d_b = first_leg(r["d"], do_ref, d_lo, d_hi)
     halo.wait_recv()
     first_block = net.me == 0
     act_ref, pre_ref, actb_ref = r["act"], r["pre"], r["actb"]
@@ -234,21 +248,6 @@
         act_ref[:, at] = act.astype(F32)
         return carry
 
-    lax.fori_loop(0, groups, conv, 0)
-
-    def legs(ref, lo, hi):
-        return (
-            (nz, net.z_of, net.at_z, cut(ref, ny, "z", lo)),
-            (ny, net.y_of, net.at_y, cut(ref, nz, "y", hi)),
-        )
-
-    w_za, w_yb = legs(wo_ref, w_lo, w_hi)
-    arrived(w_a)
-    w_a = ring_start(net, *w_za)
-    arrived(w_b)
-    w_b = ring_start(net, *w_yb)
-    d_a, d_b = first_leg(r["d"], do_ref, d_lo, d_hi)
-
     def gates(g, carry):
         at = lanes_of(g)
         gate = g_ref[:, at]
@@ -258,6 +257,7 @@
         gg_ref[:, at] = out * (s * (1.0 + gate * (1.0 - s)))
         return carry
 
+    lax.fori_loop(0, groups, conv, 0)
     lax.fori_loop(0, groups, gates, 0)
     w_a2 = ring_relay(net, *w_za, w_a)
     w_b2 = ring_relay(net, *w_yb, w_b)
@@ -323,13 +323,21 @@
 
     spread(0, b_ref)
     spread(STATE, c_ref)
+    rx_ref, row_ref, rz_ref, back_ref, edge_ref = r["rx"], r["rowt"], r["rz"], r["backt"], r["edges"]
     pe_ref, pq_ref, pack_ref, ends_ref = r["pe"], r["pq"], r["pack"], r["ends"]
     wide = (STATE, CHUNKS, LANES)
+    base1 = net.take(ny)
+
+    def pack_copy(k):
+        peer = (z * ny + lax.rem(y + k, ny), m)
+        return net.copy(pack_ref.at[lax.rem(y + k, ny)], rx_ref.at[y], base1 + k, peer)
 
     def here_of(t):
         return pl.ds(pl.multiple_of(t * CHUNKS, CHUNKS), CHUNKS)
 
-    def local(g, carry):
+    def local(i, carry):
+        k = lax.rem(i + 1, ny)
+        g = lax.rem(y + k, ny)
         at = lanes_of(g)
         pre = step_ref[:, at] + r["dbias"][:, at]
         step_ref[:, at] = jnp.maximum(pre, 0.0) + jnp.log1p(jnp.exp(-jnp.abs(pre)))
@@ -376,19 +384,22 @@
             ends_ref[pl.ds(STATE + n, 1)] = adjoint[n, 0:1]
         pack_ref[g, pl.ds(0, 2 * STATE)] = ends_ref[...].astype(BF16)
         pack_ref[g, pl.ds(2 * STATE, STATE)] = split_total(jnp.sum(total, axis=0, keepdims=True))
+
+        @pl.when(i < ny - 1)
+        def _():
+            pack_copy(k).start()
+
         return carry
 
     lax.fori_loop(0, groups, local, 0)
 
-    rx_ref, row_ref, rz_ref, back_ref, edge_ref = r["rx"], r["rowt"], r["rz"], r["backt"], r["edges"]
     fw_ref, bw_ref = r["fw"], r["bw"]
-    c1 = [net.go(pack_ref.at[net.y_of(k)], rx_ref.at[y], net.at_y(k)) for k in range(1, ny)]
     rx_ref[y] = pack_ref[y]
     my_a2 = -LOG2E * jnp.exp(alog_ref[:, lanes_of(y)])
     gb_ref, gc_ref = r["gb"], r["gc"]
     gb_ref[...] = jnp.zeros(gb_ref.shape, F32)
     gc_ref[...] = jnp.zeros(gc_ref.shape, F32)
-    arrived(c1)
+    arrived([pack_copy(k) for k in range(1, ny)])
 
     def total_of(block):
         tail = block[2 * STATE :].astype(F32)
@@ -429,28 +440,38 @@
         outof = bw_ref[j] + jnp.exp2(my_a2 * behind[j]) * tail
         back_ref[j, pl.ds(0, STATE)] = into.astype(BF16)
         back_ref[j, pl.ds(STATE, STATE)] = outof.astype(BF16)
-    c3 = [net.go(back_ref.at[net.y_of(k)], edge_ref.at[y], net.at_y(k)) for k in range(1, ny)]
+    base3 = net.take(ny)
+
+    def edge_copy(k):
+        peer = (z * ny + lax.rem(y + k, ny), m)
+        return net.copy(back_ref.at[lax.rem(y + k, ny)], edge_ref.at[y], base3 + k, peer)
+
     edge_ref[y] = back_ref[y]
-    arrived(c3)
+    for k in range(1, ny):
+        edge_copy(k).start()
 
     h_ref, mix_ref, gpre_ref, half_ref = r["h"], r["mix"], r["gpre"], r["half"]
     gas_ref, dw_ref, ra_ref, sg_ref = r["gas"], r["dw"], r["ra"], r["sg"]
-    base = net.take(groups * 8)
-
-    def dw_copy(g, k, along_z):
-        at = lanes_of(g)
+    flow_ref, slope_ref = r["flow"], r["slope"]
+    pairs = groups // 2
+    base = net.take(pairs * 8)
+
+    def dw_copy(p, k, along_z):
+        at = pl.ds(pl.multiple_of(p * 2 * LANES, 2 * LANES), 2 * LANES)
         if along_z:
             src, peer = dw_ref.at[net.z_of(k), :, :, at], net.at_z(k)
         else:
             src, peer = dw_ref.at[:, net.y_of(k), :, at], net.at_y(k)
-        return net.copy(src, ra_ref.at[k, :, :, at], base + g * 8 + k, peer)
-
-    def main(i, carry):
-        g = lax.rem(i, 2) * (groups // 2) + lax.div(i, 2)
+        return net.copy(src, ra_ref.at[k, :, :, at], base + p * 8 + k, peer)
+
+    def main(g):
         at = lanes_of(g)
-        rates = -jnp.exp(alog_ref[:, at])
-        a1 = jnp.broadcast_to(rates[:, None, :], wide)
-        a2 = a1 * LOG2E
+
+        @pl.when(g != y)
+        def _():
+            edge_copy(lax.rem(y - g + ny, ny)).wait_recv()
+
+        a2 = jnp.broadcast_to((-LOG2E * jnp.exp(alog_ref[:, at]))[:, None, :], wide)
         skip = skip_ref[:, at]
         total = jnp.sum(stacked(step_ref[:, at]), axis=0)[None]
         left, right = total, total
@@ -480,57 +501,91 @@
             mix_ref[here] = mixed * gg_ref[here, at]
             return state
 
-        lax.fori_loop(0, tics, ahead, state, unroll=2)
+        lax.fori_loop(0, tics, ahead, state, unroll=UNROLL_F)
         r["mixo"][:, at] = mix_ref[...].astype(BF16)
-
-        def back(i, carry):
-            adjoint, rate_sum, pre_sum, skip_sum = carry
-            t = tics - 1 - i
-            here = here_of(t)
-            step = step_ref[here, at]
-            act = act_ref[here, at]
-            grad = g_ref[here, at]
-            lam = c_ref[t] * grad[None] + adjoint
-            adjoint = jnp.exp2(step[None] * a2) * lam
-            pull = adjoint * h_ref[t]
-            gc_ref[t] += h_ref[t + 1] * grad[None]
-            gb_ref[t] += lam * (step * act)[None]
-            flow = jnp.sum(lam * b_ref[t], axis=0)
-            slope = jnp.sum(pull * a1, axis=0)
-            gas_ref[here, at] = flow * step + skip * grad
-            pre = (flow * act + slope) * sig_ref[here, at]
-            gpre_ref[here] = pre
-            return (adjoint, rate_sum + pull * step[None], pre_sum + pre, skip_sum + grad * act)
-
         none = jnp.zeros((CHUNKS, LANES), F32)
-        _, rate_sum, pre_sum, skip_sum = lax.fori_loop(
-            0, tics, back, (adjoint, jnp.zeros(wide, F32), none, none)
+        pre_sum, skip_sum = none, none
+        span = STATE // SPLIT
+        for part in range(SPLIT):
+            of = slice(part * span, part * span + span)
+            ns = pl.ds(part * span, span)
+            a2_part = a2[of]
+            opening, closing = part == 0, part == SPLIT - 1
+
+            def back(i, carry):
+                adjoint, rate_sum, pre_sum, skip_sum = carry
+                t = tics - 1 - i
+                here = here_of(t)
+                step = step_ref[here, at]
+                act = act_ref[here, at]
+                grad = g_ref[here, at]
+                lam = c_ref[t, ns] * grad[None] + adjoint
+                adjoint = jnp.exp2(step[None] * a2_part) * lam
+                pull = adjoint * h_ref[t, ns]
+                gc_ref[t, ns] += h_ref[t + 1, ns] * grad[None]
+                gb_ref[t, ns] += lam * (step * act)[None]
+                slopes = pull * a2_part
+                flow = jnp.sum(lam * b_ref[t, ns], axis=0)
+                slope = jnp.sum(slopes, axis=0)
+                if not opening:
+                    flow = flow + flow_ref[here]
+                    slope = slope + slope_ref[here]
+                if closing:
+                    gas_ref[here, at] = flow * step + skip * grad
+                    pre = (flow * act + slope * LN2) * sig_ref[here, at]
+                    gpre_ref[here] = pre
+                    pre_sum = pre_sum + pre
+                    skip_sum = skip_sum + grad * act
+                else:
+                    flow_ref[here] = flow
+                    slope_ref[here] = slope
+                return (adjoint, rate_sum + slopes * step[None], pre_sum, skip_sum)
+
+            _, rate_sum, pre_sum, skip_sum = lax.fori_loop(
+                0,
+                tics,
+                back,
+                (adjoint[of], jnp.zeros((span, CHUNKS, LANES), F32), pre_sum, skip_sum),
+                unroll=UNROLL_B,
+            )
+            for n in range(span):
+                sg_ref[g, pl.ds(CHUNKS + part * span + n, 1)] = LN2 * jnp.sum(
+                    rate_sum[n], axis=0, keepdims=True
+                )
+        half_ref[:, at] = gpre_ref[...].astype(BF16)
+        sg_ref[g, pl.ds(0, 1)] = jnp.sum(pre_sum, axis=0, keepdims=True)
+        sg_ref[g, pl.ds(1, 1)] = jnp.sum(skip_sum, axis=0, keepdims=True)
+        sg_ref[g, pl.ds(2, CHUNKS - 2)] = jnp.zeros((CHUNKS - 2, LANES), F32)
+
+    def main_pair(i, carry):
+        turn = lax.rem(i, 2) * (pairs // 2) + lax.div(i, 2)
+        p = lax.rem(lax.div(y, 2) + turn, pairs)
+
+        def one(j, carry):
+            main(2 * p + lax.rem(y + j, 2))
+            return carry
+
+        lax.fori_loop(0, 2, one, 0)
+        at = pl.ds(pl.multiple_of(p * 2 * LANES, 2 * LANES), 2 * LANES)
+        dw_ref[:, :, :, at] = (
+            dot(r["low_t"][...], half_ref[:, at])
+            .reshape(dw_ref.shape[:3] + (2 * LANES,))
+            .astype(BF16)
         )
-        half = gpre_ref[...].astype(BF16)
-        half_ref[:, at] = half
-        dw_ref[:, :, :, at] = (
-            dot(r["low_t"][...], half).reshape(dw_ref.shape[:3] + (LANES,)).astype(BF16)
-        )
-
-        @pl.when(g < groups // 2)
+
+        @pl.when(p < pairs // 2)
         def _():
             for k in range(1, nz):
-                dw_copy(g, k, True).start()
-
-        @pl.when(g >= groups // 2)
+                dw_copy(p, k, True).start()
+
+        @pl.when(p >= pairs // 2)
         def _():
             for k in range(1, ny):
-                dw_copy(g, k, False).start()
-
-        sg_ref[g] = jnp.zeros(sg_ref.shape[1:], F32)
-        sg_ref[g, pl.ds(5, 1)] = jnp.sum(pre_sum, axis=0, keepdims=True)
-        sg_ref[g, pl.ds(6, 1)] = jnp.sum(skip_sum, axis=0, keepdims=True)
-        rate_sum = rate_sum * a1
-        for n in range(STATE):
-            sg_ref[g, pl.ds(CHUNKS + n, 1)] = jnp.sum(rate_sum[n], axis=0, keepdims=True)
+                dw_copy(p, k, False).start()
+
         return carry
 
-    lax.fori_loop(0, groups, main, 0)
+    lax.fori_loop(0, pairs, main_pair, 0)
 
     pick = jnp.where(
         lax.broadcasted_iota(jnp.int32, (STATE * LANES, STATE), 0) // LANES
@@ -552,9 +607,9 @@
         .reshape(sum_shape[:2] + (2 * STATE,))
     )
     s3 = sum_start(r["p2"], r["q2"])
+    t1 = [net.go(sg_ref.at[net.z_of(k)], r["sr"].at[k], net.at_z(k)) for k in range(1, nz)]
     sa_ref, sb_ref, rra_ref, rrb_ref = r["sa"], r["sb"], r["rra"], r["rrb"]
     lo, hi = pl.ds(0, half_width), pl.ds(half_width, half_width)
-    half_groups = groups // 2
 
     def add_a(i, carry):
         total = dw_ref[z, i, :, lo].astype(F32)
@@ -571,15 +626,21 @@
         return carry
 
     s4 = sum_turn(s3, r["p2"], r["q2"], r["acc2"], r["gproj"])
-    arrived([dw_copy(g, k, True) for g in range(half_groups) for k in range(1, nz)])
+    arrived([dw_copy(p, k, True) for p in range(pairs // 2) for k in range(1, nz)])
     lax.fori_loop(0, ny, add_a, 0)
     a2nd = [net.go(sa_ref.at[net.y_of(k)], rra_ref.at[k], net.at_y(k)) for k in range(1, ny)]
-    arrived([dw_copy(g, k, False) for g in range(half_groups, groups) for k in range(1, ny)])
+    arrived([dw_copy(p, k, False) for p in range(pairs // 2, pairs) for k in range(1, ny)])
     lax.fori_loop(0, nz, add_b, 0)
     b2nd = [net.go(sb_ref.at[net.z_of(k)], rrb_ref.at[k], net.at_z(k)) for k in range(1, nz)]
+    arrived(t1)
+    total = sg_ref[z]
+    for k in range(1, nz):
+        total = total + r["sr"][k]
+    r["ss"][...] = total
+    t2 = [net.go(r["ss"], r["srr"].at[k], net.at_y(k)) for k in range(1, ny)]
     arrived(s4)
 
-    out_ref, head_ref = r["grad"], r["head"]
+    out_ref, head_ref, cg_ref = r["grad"], r["head"], r["cg"]
     out_ref[...] = dot(r["gproj"][...].reshape(tokens, PROJ), wo_ref[...].reshape(width, PROJ), ((1,), (1,)))
 
     def close(g, carry):
@@ -594,16 +655,17 @@
         padded = with_earlier(x, edge, CONV - 1)
         for k in range(CONV):
             part = jnp.sum(grad * padded[k : k + x.shape[0]], axis=0)
-            sg_ref[g, pl.ds(k, 1)] = jnp.sum(part, axis=0, keepdims=True)
-        sg_ref[g, pl.ds(CONV, 1)] = jnp.sum(jnp.sum(grad, axis=0), axis=0, keepdims=True)
+            cg_ref[g, pl.ds(k, 1)] = jnp.sum(part, axis=0, keepdims=True)
+        cg_ref[g, pl.ds(CONV, 1)] = jnp.sum(jnp.sum(grad, axis=0), axis=0, keepdims=True)
+        cg_ref[g, pl.ds(CONV + 1, 3)] = jnp.zeros((3, LANES), F32)
         head_ref[:, at] = jnp.zeros((CHUNKS, LANES), F32)
         for k in range(CONV - 1):
             head_ref[pl.ds(k, 1), at] = grad[k, 0:1]
         return carry
 
     lax.fori_loop(0, groups, close, 0)
-    t1 = [net.go(sg_ref.at[net.z_of(k)], r["sr"].at[k], net.at_z(k)) for k in range(1, nz)]
     later = net.go(head_ref, r["later"], net.at_ctx(-1))
+    u1 = [net.go(cg_ref.at[net.z_of(k)], r["cr"].at[k], net.at_z(k)) for k in range(1, nz)]
     arrived(a2nd)
     total = sa_ref[y].astype(F32)
     for k in range(1, ny):
@@ -614,31 +676,54 @@
     for k in range(1, nz):
         total = total + rrb_ref[k].astype(F32)
     r["dwo"][:, hi] = total
-    arrived(t1)
-    total = sg_ref[z]
-    for k in range(1, nz):
-        total = total + r["sr"][k]
-    r["ss"][...] = total
-    t2 = [net.go(r["ss"], r["srr"].at[k], net.at_y(k)) for k in range(1, ny)]
-    later.wait_recv()
     arrived(t2)
     total = r["ss"][...]
     for k in range(1, ny):
         total = total + r["srr"][k]
-    r["smallo"][...] = total
-    for g in range(groups):
-        along_z = g < half_groups
+    r["smallo"][pl.ds(CHUNKS, 24)] = total
+    arrived(u1)
+    total = cg_ref[z]
+    for k in range(1, nz):
+        total = total + r["cr"][k]
+    r["cs"][...] = total
+    u2 = [net.go(r["cs"], r["crr"].at[k], net.at_y(k)) for k in range(1, ny)]
+    later.wait_recv()
+    last_block = net.me == n_ctx - 1
+
+    def conv_back(g, carry):
+        at = lanes_of(g)
+        grad = stacked(out_ref[:, at])
+        edge = jnp.where(last_block, 0.0, r["later"][:, at])
+        rest = pltpu.roll(grad[: CONV - 1], CHUNKS - 1, 1)
+        rest = jnp.where(row == CHUNKS - 1, edge[: CONV - 1][:, None, :], rest)
+        padded = jnp.concatenate([grad, rest], axis=0)
+        taps = r["cw"][:, at]
+        total = taps[CONV - 1 :][None] * grad
+        for k in range(CONV - 1):
+            off = CONV - 1 - k
+            total = total + taps[k : k + 1][None] * padded[off : off + grad.shape[0]]
+        r["seqo"][:, at] = flat(total).astype(BF16)
+        return carry
+
+    lax.fori_loop(0, groups, conv_back, 0)
+    for k in range(1, ny):
+        pack_copy(k).wait_send()
+        edge_copy(k).wait_send()
+    for p in range(pairs):
+        along_z = p < pairs // 2
         for k in range(1, nz if along_z else ny):
-            dw_copy(g, k, along_z).wait_send()
+            dw_copy(p, k, along_z).wait_send()
+    arrived(u2)
+    total = r["cs"][...]
+    for k in range(1, ny):
+        total = total + r["crr"][k]
+    r["smallo"][pl.ds(0, CHUNKS)] = total
     net.finish()
 
 
 def end_kernel(
-    n_ctx,
     ny,
-    grad_ref,
-    halo_ref,
-    cw_ref,
+    seq_ref,
     mix_ref,
     dwo_ref,
     small_ref,
@@ -650,41 +735,21 @@
     t_ref,
     a_ref,
     s_ref,
-    sum_ref,
 ):
-    tokens, width = grad_ref.shape
+    tokens, width = seq_ref.shape
     me = lax.axis_index("ctx")
-    last = me == n_ctx - 1
-
-    def group(g, carry):
-        at = lanes_of(g)
-        grad = stacked(grad_ref[:, at])
-        edge = jnp.where(last, 0.0, halo_ref[:, at])
-        later = pltpu.roll(grad[: CONV - 1], CHUNKS - 1, 1)
-        later = jnp.where(chunk_row() == CHUNKS - 1, edge[: CONV - 1][:, None, :], later)
-        padded = jnp.concatenate([grad, later], axis=0)
-        taps = cw_ref[:, at]
-        total = taps[CONV - 1 :][None] * grad
-        for k in range(CONV - 1):
-            off = CONV - 1 - k
-            total = total + taps[k : k + 1][None] * padded[off : off + grad.shape[0]]
-        sum_ref[:, at] = flat(total).astype(BF16)
-        return carry
-
-    lax.fori_loop(0, width // LANES, group, 0)
     unperm = permutation(tokens, True).astype(BF16)
-    out_ref[...] = dot(unperm, sum_ref[...]).astype(BF16)
+    out_ref[...] = dot(unperm, seq_ref[...]).astype(BF16)
     gate_ref[...] = dot(unperm, mix_ref[...]).astype(BF16)
     dw_ref[...] = dwo_ref[...]
     share = LANES // ny
-    mine = small_ref[...]
     shift = lax.rem(LANES - lax.rem(me, ny) * share, LANES)
-    mine = pltpu.roll(mine, shift, 1)[:, :share]
+    mine = pltpu.roll(small_ref[...], shift, 1)[:, :share]
     w_ref[...] = mine[:CONV]
     b_ref[...] = mine[CONV : CONV + 1]
-    t_ref[...] = mine[5:6]
-    s_ref[...] = mine[6:7]
-    a_ref[...] = mine[CHUNKS:]
+    t_ref[...] = mine[CHUNKS : CHUNKS + 1]
+    s_ref[...] = mine[CHUNKS + 1 : CHUNKS + 2]
+    a_ref[...] = mine[2 * CHUNKS :]
 
 
 def body(
@@ -722,11 +787,10 @@
         skip=skip_gain.reshape(line),
     )
     outs = dict(
-        grad=(full, F32),
-        later=((CHUNKS, width), F32),
+        seqo=(full, BF16),
         mixo=(full, BF16),
         dwo=((rows, width), F32),
-        smallo=((24, LANES), F32),
+        smallo=((24 + CHUNKS, LANES), F32),
     )
     part = (n_mp, tokens // n_mp, PROJ)
     scratch = dict(
@@ -782,10 +846,18 @@
         ss=((24, LANES), F32),
         srr=((ny, 24, LANES), F32),
         head=((CHUNKS, width), F32),
+        later=((CHUNKS, width), F32),
+        grad=(full, F32),
+        flow=((tokens, LANES), F32),
+        slope=((tokens, LANES), F32),
+        cg=((groups, CHUNKS, LANES), F32),
+        cr=((nz, CHUNKS, LANES), F32),
+        cs=((CHUNKS, LANES), F32),
+        crr=((ny, CHUNKS, LANES), F32),
     )
     names = list(inputs) + list(outs) + list(scratch) + ["send", "recv"]
     slots = 256
-    grad, later, mix, dwo, small = call(
+    seq, mix, dwo, small = call(
         functools.partial(mega_kernel, nz, ny, n_ctx, n_mp, names),
         list(outs.values()),
         list(inputs.values()),
@@ -795,7 +867,7 @@
     )
     share = LANES // ny
     grad_seq, grad_gate, grad_dtw, g_w, g_b, g_t, g_a, g_s = call(
-        functools.partial(end_kernel, n_ctx, ny),
+        functools.partial(end_kernel, ny),
         [
             (full, BF16),
             (full, BF16),
@@ -806,8 +878,7 @@
             ((STATE, share), F32),
             ((1, share), F32),
         ],
-        [grad, later, conv_weight, mix, dwo, small],
-        [pltpu.VMEM(full, BF16)],
+        [seq, mix, dwo, small],
     )
     return (
         grad_seq,

time: 108 us -> 98.4 us (0.911)
  Pallas kernels: 106 us -> 96.6 us
    pallas_call x2, Pallas kernels: 106 us -> 96.6 us  [call(): pl.pallas_call(kernel, out_shape=tuple((jax.ShapeDtypeStruct(s, d) for s,...]
where the time goes in v3:
time: 98.4 us; the launch traced here: 97.3 us
  Pallas kernels  96.6 us (98%)
    pallas_call x2, Pallas kernels, call(): pl.pallas_call(kernel, out_shape=tuple((jax.ShapeDtypeStruct(s, d) for s,...  96.6 us

profile of v3, /device:TPU:6, one launch (start us, length us, event | category | flops | bytes accessed | tf_op | source)
XLA Modules:
  0.0 97.3 jit_solution(16920969505635824543)
XLA Ops:
  0.6 94.6 %shard_map.170 = (bf16[128,1024]{1,0:T(8,128)(2,1)}, bf16[128,1024]{1,0:T(8,128)(2,1)}, f32[8,1024]{1,0:T(8,128)}, f32[32,128]{1,0:T(8,128)}) custom-call(bf16[128,1024]{1,0:T(8,128)(2,1)} %refs_0_.1, bf16[128,1024]{1,0:T(8,128)(2,1)} %refs_1_.1, bf16[128,1024]{1,0:T(8,128)(2,1)} %refs_2_.1, s32[1,128]{1,0:T(1,128)} %bitcast.10, f32[4,1024]{1,0:T(4,128)} %refs_4_.1, ...), custom_call_target="tpu_custom_call" | custom-call | tf_op jit(solution)/shard_map/pallas_call | solution.py:35
  95.2 2.1 %shard_map.171 = (bf16[128,1024]{1,0:T(8,128)(2,1)}, bf16[128,1024]{1,0:T(8,128)(2,1)}, f32[8,1024]{1,0:T(8,128)}, f32[4,16]{1,0:T(4,128)}, f32[1,16]{1,0:T(1,12...) custom-call(bf16[128,1024]{1,0:T(8,128)(2,1)} %get-tuple-element.20.seq_ref, ...), custom_call_target="tpu_custom_call" | custom-call | tf_op jit(solution)/shard_map/pallas_call | solution.py:35

commit v4 on v3

--- a/solution.py
+++ b/solution.py
@@ -17,8 +17,9 @@
 LOG2E = 1.4426950408889634
 LN2 = 0.6931471805599453
 SPLIT = 2
-UNROLL_F = 2
-UNROLL_B = 2
+UNROLL_F = 4
+UNROLL_B = 4
+UNROLL_L = 4
 MESH = pl.DeviceIdType.MESH
 F32, BF16 = jnp.float32, jnp.bfloat16
 VMEM = pl.BlockSpec(memory_space=pltpu.VMEM)
@@ -174,6 +175,30 @@
     return made
 
 
+def hop_start(net, size, place, peer, part):
+    ks = (1, -1) if size == 8 else range(1, size)
+    return [net.go(part(place(0), 2), part(place(0), 2), peer(k)) for k in ks]
+
+
+def hop_next(net, size, place, peer, part, first):
+    arrived(first)
+    if size != 8:
+        return []
+    return [net.go(part(place(-k), 2), part(place(-k), 2), peer(k)) for k in (1, -1)]
+
+
+def hop_last(net, size, place, peer, part, first):
+    arrived(first)
+    if size != 8:
+        return []
+    return [
+        net.go(part(place(-2), 0), part(place(-2), 0), peer(2)),
+        net.go(part(place(2), 1), part(place(2), 1), peer(-2)),
+        net.go(part(place(-2), 2), part(place(-2), 2), peer(1)),
+        net.go(part(place(2), 2), part(place(2), 2), peer(-1)),
+    ]
+
+
 def cut(ref, size, axis, lanes):
     def part(origin, which):
         span = pl.ds(0, size) if which == 2 else pl.ds(which * (size // 2), size // 2)
@@ -206,8 +231,17 @@
         b = [net.go(src.at[:, hi], ref.at[z, y, :, hi], net.at_z(k)) for k in range(1, nz)]
         return a, b
 
+    def legs(ref, lo, hi):
+        return (
+            (nz, net.z_of, net.at_z, cut(ref, ny, "z", lo)),
+            (ny, net.y_of, net.at_y, cut(ref, nz, "y", hi)),
+        )
+
+    w_za, w_yb = legs(wo_ref, w_lo, w_hi)
+    d_za, d_yb = legs(do_ref, d_lo, d_hi)
     w_a, w_b = first_leg(r["w"], wo_ref, w_lo, w_hi)
     halo = net.go(seq_ref.at[pl.ds(tokens - 16, 16)], r["halo"], net.at_ctx(1))
+    d_a, d_b = first_leg(r["d"], do_ref, d_lo, d_hi)
     perm = permutation(tokens)
     signed = (perm * -r["flag"][...].astype(F32)).astype(BF16)
     perm = perm.astype(BF16)
@@ -216,18 +250,14 @@
     gg_ref[...] = dot(signed, r["up"][...])
     wo_ref[z, y] = r["w"][...]
     do_ref[z, y] = r["d"][...]
-    def legs(ref, lo, hi):
-        return (
-            (nz, net.z_of, net.at_z, cut(ref, ny, "z", lo)),
-            (ny, net.y_of, net.at_y, cut(ref, nz, "y", hi)),
-        )
-
-    w_za, w_yb = legs(wo_ref, w_lo, w_hi)
     arrived(w_a)
     w_a = ring_start(net, *w_za)
     arrived(w_b)
     w_b = ring_start(net, *w_yb)
-    d_a, d_b = first_leg(r["d"], do_ref, d_lo, d_hi)
+    arrived(d_a)
+    d_a = hop_start(net, *d_za)
+    arrived(d_b)
+    d_b = hop_start(net, *d_yb)
     halo.wait_recv()
     first_block = net.me == 0
     act_ref, pre_ref, actb_ref = r["act"], r["pre"], r["actb"]
@@ -261,11 +291,8 @@
     lax.fori_loop(0, groups, gates, 0)
     w_a2 = ring_relay(net, *w_za, w_a)
     w_b2 = ring_relay(net, *w_yb, w_b)
-    d_za, d_yb = legs(do_ref, d_lo, d_hi)
-    arrived(d_a)
-    d_a = ring_start(net, *d_za)
-    arrived(d_b)
-    d_b = ring_start(net, *d_yb)
+    d_a = hop_next(net, *d_za, d_a)
+    d_b = hop_next(net, *d_yb, d_b)
     if nz == 8:
         arrived(w_a[2:])
     if ny == 8:
@@ -289,14 +316,10 @@
         return [net.go(acc_ref, o_ref.at[m], net.at_m(k)) for k in range(1, n_mp)]
 
     s1 = sum_start(r["p1"], r["q1"])
-    d_a2 = ring_relay(net, *d_za, d_a)
-    d_b2 = ring_relay(net, *d_yb, d_b)
+    d_a = hop_last(net, *d_za, d_a)
+    d_b = hop_last(net, *d_yb, d_b)
     s2 = sum_turn(s1, r["p1"], r["q1"], r["acc1"], r["proj"])
-    if nz == 8:
-        arrived(d_a[2:])
-    if ny == 8:
-        arrived(d_b[2:])
-    arrived(d_a2 + d_b2)
+    arrived(d_a + d_b)
 
     def lay_out(i, carry):
         rows = do_ref.shape[2] * ny
@@ -311,7 +334,6 @@
     proj = r["proj"][...].reshape(tokens, PROJ)
     low = proj[:, :RANK]
     cols = proj[:, RANK:].astype(F32)
-    r["low_t"][...] = low.astype(F32).T.astype(BF16)
     step_ref, sig_ref = r["step"], r["sig"]
     step_ref[...] = dot(low, dt_ref[...])
     b_ref, c_ref = r["b"], r["c"]
@@ -324,6 +346,7 @@
     spread(0, b_ref)
     spread(STATE, c_ref)
     rx_ref, row_ref, rz_ref, back_ref, edge_ref = r["rx"], r["rowt"], r["rz"], r["backt"], r["edges"]
+    decay_ref = r["decay"]
     pe_ref, pq_ref, pack_ref, ends_ref = r["pe"], r["pq"], r["pack"], r["ends"]
     wide = (STATE, CHUNKS, LANES)
     base1 = net.take(ny)
@@ -335,36 +358,28 @@
     def here_of(t):
         return pl.ds(pl.multiple_of(t * CHUNKS, CHUNKS), CHUNKS)
 
-    def local(i, carry):
-        k = lax.rem(i + 1, ny)
-        g = lax.rem(y + k, ny)
+    run_ref, total_ref, wl_ref, wr_ref = r["run"], r["total"], r["wl"], r["wr"]
+
+    def others(total):
+        left, right = total, total
+        shift = 1
+        while shift < CHUNKS:
+            left = left + jnp.where(row >= shift, pltpu.roll(left, shift, 1), 0.0)
+            right = right + jnp.where(
+                row < CHUNKS - shift, pltpu.roll(right, CHUNKS - shift, 1), 0.0
+            )
+            shift *= 2
+        before = jnp.where(row >= 1, pltpu.roll(left, 1, 1), 0.0)
+        after = jnp.where(row < CHUNKS - 1, pltpu.roll(right, CHUNKS - 1, 1), 0.0)
+        return before, after
+
+    def settle(g, carry):
         at = lanes_of(g)
-        pre = step_ref[:, at] + r["dbias"][:, at]
-        step_ref[:, at] = jnp.maximum(pre, 0.0) + jnp.log1p(jnp.exp(-jnp.abs(pre)))
-        sig_ref[:, at] = sigmoid(pre)
         a2 = jnp.broadcast_to((-LOG2E * jnp.exp(alog_ref[:, at]))[:, None, :], wide)
-
-        def ahead(t, carry):
-            state, total = carry
-            here = here_of(t)
-            step = step_ref[here, at]
-            flow = step * act_ref[here, at]
-            state = jnp.exp2(step[None] * a2) * state + b_ref[t] * flow[None]
-            return state, total + step
-
-        zero = jnp.zeros(wide, F32)
-        state, total = lax.fori_loop(
-            0, tics, ahead, (zero, jnp.zeros((CHUNKS, LANES), F32)), unroll=4
-        )
-
-        def back(i, adjoint):
-            t = tics - 1 - i
-            here = here_of(t)
-            step = step_ref[here, at]
-            return jnp.exp2(step[None] * a2) * (c_ref[t] * g_ref[here, at][None] + adjoint)
-
-        adjoint = lax.fori_loop(0, tics, back, zero, unroll=4)
-        left = jnp.exp2(total[None] * a2)
+        earlier, later = others(total_ref[:, at][None])
+        wl_ref[:, :, at] = jnp.exp2(a2 * earlier)
+        wr_ref[:, :, at] = jnp.exp2(a2 * later)
+        state, adjoint, left = pe_ref[:, :, at], pq_ref[:, :, at], run_ref[:, :, at]
         right = left
         shift = 1
         while shift < CHUNKS:
@@ -377,11 +392,46 @@
             )
             right = right * jnp.where(in_right, pltpu.roll(right, CHUNKS - shift, 1), 1.0)
             shift *= 2
+        pe_ref[:, :, at] = jnp.where(row >= 1, pltpu.roll(state, 1, 1), 0.0)
+        pq_ref[:, :, at] = jnp.where(row < CHUNKS - 1, pltpu.roll(adjoint, CHUNKS - 1, 1), 0.0)
+        return carry
+
+    def local(i, carry):
+        k = lax.rem(i + 1, ny)
+        g = lax.rem(y + k, ny)
+        at = lanes_of(g)
+        pre = step_ref[:, at] + r["dbias"][:, at]
+        step_ref[:, at] = jnp.maximum(pre, 0.0) + jnp.log1p(jnp.exp(-jnp.abs(pre)))
+        sig_ref[:, at] = pre
+        a2 = jnp.broadcast_to((-LOG2E * jnp.exp(alog_ref[:, at]))[:, None, :], wide)
+
+        def ahead(t, carry):
+            state, adjoint, run, total = carry
+            here = here_of(t)
+            step = step_ref[here, at]
+            flow = step * act_ref[here, at]
+            decay = jnp.exp2(step[None] * a2)
+            decay_ref[g, t] = decay
+            run = run * decay
+            state = decay * state + b_ref[t] * flow[None]
+            adjoint = adjoint + run * (c_ref[t] * g_ref[here, at][None])
+            return state, adjoint, run, total + step
+
+        zero = jnp.zeros(wide, F32)
+        state, adjoint, left, total = lax.fori_loop(
+            0,
+            tics,
+            ahead,
+            (zero, zero, jnp.ones(wide, F32), jnp.zeros((CHUNKS, LANES), F32)),
+            unroll=UNROLL_L,
+        )
         pe_ref[:, :, at] = state
         pq_ref[:, :, at] = adjoint
-        for n in range(STATE):
-            ends_ref[pl.ds(n, 1)] = state[n, CHUNKS - 1 : CHUNKS]
-            ends_ref[pl.ds(STATE + n, 1)] = adjoint[n, 0:1]
+        run_ref[:, :, at] = left
+        total_ref[:, at] = total
+        earlier, later = others(total[None])
+        ends_ref[pl.ds(0, STATE)] = jnp.sum(state * jnp.exp2(a2 * later), axis=1)
+        ends_ref[pl.ds(STATE, STATE)] = jnp.sum(adjoint * jnp.exp2(a2 * earlier), axis=1)
         pack_ref[g, pl.ds(0, 2 * STATE)] = ends_ref[...].astype(BF16)
         pack_ref[g, pl.ds(2 * STATE, STATE)] = split_total(jnp.sum(total, axis=0, keepdims=True))
 
@@ -397,6 +447,14 @@
     rx_ref[y] = pack_ref[y]
     my_a2 = -LOG2E * jnp.exp(alog_ref[:, lanes_of(y)])
     gb_ref, gc_ref = r["gb"], r["gc"]
+    r["low_t"][...] = low.astype(F32).T.astype(BF16)
+
+    def slopes(g, carry):
+        at = lanes_of(g)
+        sig_ref[:, at] = sigmoid(sig_ref[:, at])
+        return carry
+
+    lax.fori_loop(0, groups, slopes, 0)
     gb_ref[...] = jnp.zeros(gb_ref.shape, F32)
     gc_ref[...] = jnp.zeros(gc_ref.shape, F32)
     arrived([pack_copy(k) for k in range(1, ny)])
@@ -425,6 +483,7 @@
     row_ref[pl.ds(2 * STATE, STATE)] = split_total(sums)
     c2 = [net.go(row_ref, rz_ref.at[z], net.at_z(k)) for k in range(1, nz)]
     rz_ref[z] = row_ref[...]
+    lax.fori_loop(0, groups, settle, 0)
     arrived(c2)
     head, tail = zero, zero
     for k in range(nz):
@@ -452,17 +511,21 @@
 
     h_ref, mix_ref, gpre_ref, half_ref = r["h"], r["mix"], r["gpre"], r["half"]
     gas_ref, dw_ref, ra_ref, sg_ref = r["gas"], r["dw"], r["ra"], r["sg"]
-    flow_ref, slope_ref = r["flow"], r["slope"]
+    rs_ref, ps_ref = r["rs"], r["ps"]
+    flow_ref, slope_ref, low_ref = r["flow"], r["slope"], r["low_sum"]
+    low_ref[...] = jnp.zeros(low_ref.shape, F32)
     pairs = groups // 2
-    base = net.take(pairs * 8)
+    base = net.take(pairs * 16)
 
     def dw_copy(p, k, along_z):
-        at = pl.ds(pl.multiple_of(p * 2 * LANES, 2 * LANES), 2 * LANES)
         if along_z:
+            at = lanes_of(2 * p)
             src, peer = dw_ref.at[net.z_of(k), :, :, at], net.at_z(k)
         else:
+            at = lanes_of(2 * p + 1)
             src, peer = dw_ref.at[:, net.y_of(k), :, at], net.at_y(k)
-        return net.copy(src, ra_ref.at[k, :, :, at], base + p * 8 + k, peer)
+        slot = base + p * 16 + k + (0 if along_z else 8)
+        return net.copy(src, ra_ref.at[k, :, :, at], slot, peer)
 
     def main(g):
         at = lanes_of(g)
@@ -473,29 +536,18 @@
 
         a2 = jnp.broadcast_to((-LOG2E * jnp.exp(alog_ref[:, at]))[:, None, :], wide)
         skip = skip_ref[:, at]
-        total = jnp.sum(stacked(step_ref[:, at]), axis=0)[None]
-        left, right = total, total
-        shift = 1
-        while shift < CHUNKS:
-            left = left + jnp.where(row >= shift, pltpu.roll(left, shift, 1), 0.0)
-            right = right + jnp.where(
-                row < CHUNKS - shift, pltpu.roll(right, CHUNKS - shift, 1), 0.0
-            )
-            shift *= 2
         ends = edge_ref[g].astype(F32)
         into = jnp.broadcast_to(ends[:STATE][:, None, :], wide)
         outof = jnp.broadcast_to(ends[STATE:][:, None, :], wide)
-        state = jnp.where(row >= 1, pltpu.roll(pe_ref[:, :, at], 1, 1), 0.0)
-        state = state + jnp.exp2(a2 * (left - total)) * into
-        adjoint = jnp.where(row < CHUNKS - 1, pltpu.roll(pq_ref[:, :, at], CHUNKS - 1, 1), 0.0)
-        adjoint = adjoint + jnp.exp2(a2 * (right - total)) * outof
+        state = pe_ref[:, :, at] + wl_ref[:, :, at] * into
+        adjoint = pq_ref[:, :, at] + wr_ref[:, :, at] * outof
         h_ref[0] = state
 
         def ahead(t, state):
             here = here_of(t)
             step = step_ref[here, at]
             act = act_ref[here, at]
-            state = jnp.exp2(step[None] * a2) * state + b_ref[t] * (step * act)[None]
+            state = decay_ref[g, t] * state + b_ref[t] * (step * act)[None]
             h_ref[t + 1] = state
             mixed = jnp.sum(c_ref[t] * state, axis=0) + skip * act
             mix_ref[here] = mixed * gg_ref[here, at]
@@ -520,7 +572,7 @@
                 act = act_ref[here, at]
                 grad = g_ref[here, at]
                 lam = c_ref[t, ns] * grad[None] + adjoint
-                adjoint = jnp.exp2(step[None] * a2_part) * lam
+                adjoint = decay_ref[g, t, ns] * lam
                 pull = adjoint * h_ref[t, ns]
                 gc_ref[t, ns] += h_ref[t + 1, ns] * grad[None]
                 gb_ref[t, ns] += lam * (step * act)[None]
@@ -548,14 +600,17 @@
                 (adjoint[of], jnp.zeros((span, CHUNKS, LANES), F32), pre_sum, skip_sum),
                 unroll=UNROLL_B,
             )
-            for n in range(span):
-                sg_ref[g, pl.ds(CHUNKS + part * span + n, 1)] = LN2 * jnp.sum(
-                    rate_sum[n], axis=0, keepdims=True
-                )
+            rs_ref[g, ns] = rate_sum
         half_ref[:, at] = gpre_ref[...].astype(BF16)
-        sg_ref[g, pl.ds(0, 1)] = jnp.sum(pre_sum, axis=0, keepdims=True)
-        sg_ref[g, pl.ds(1, 1)] = jnp.sum(skip_sum, axis=0, keepdims=True)
+        ps_ref[g, 0] = pre_sum
+        ps_ref[g, 1] = skip_sum
+
+    def gather_sums(g, carry):
+        sg_ref[g, pl.ds(0, 1)] = jnp.sum(ps_ref[g, 0], axis=0, keepdims=True)
+        sg_ref[g, pl.ds(1, 1)] = jnp.sum(ps_ref[g, 1], axis=0, keepdims=True)
         sg_ref[g, pl.ds(2, CHUNKS - 2)] = jnp.zeros((CHUNKS - 2, LANES), F32)
+        sg_ref[g, pl.ds(CHUNKS, STATE)] = LN2 * jnp.sum(rs_ref[g], axis=1)
+        return carry
 
     def main_pair(i, carry):
         turn = lax.rem(i, 2) * (pairs // 2) + lax.div(i, 2)
@@ -573,16 +628,11 @@
             .astype(BF16)
         )
 
-        @pl.when(p < pairs // 2)
-        def _():
-            for k in range(1, nz):
-                dw_copy(p, k, True).start()
-
-        @pl.when(p >= pairs // 2)
-        def _():
-            for k in range(1, ny):
-                dw_copy(p, k, False).start()
-
+        for k in range(1, nz):
+            dw_copy(p, k, True).start()
+        for k in range(1, ny):
+            dw_copy(p, k, False).start()
+        low_ref[...] += dot(half_ref[:, at], dt_ref[:, at], ((1,), (1,)))
         return carry
 
     lax.fori_loop(0, pairs, main_pair, 0)
@@ -599,7 +649,7 @@
         return dot(side.astype(BF16), pick)
 
     r["p2"][:, :, pl.ds(0, RANK)] = (
-        dot(half_ref[...], dt_ref[...], ((1,), (1,))).astype(BF16).reshape(sum_shape[:2] + (RANK,))
+        low_ref[...].astype(BF16).reshape(sum_shape[:2] + (RANK,))
     )
     r["p2"][:, :, pl.ds(RANK, 2 * STATE)] = (
         jnp.concatenate([folded(gb_ref), folded(gc_ref)], axis=1)
@@ -607,29 +657,33 @@
         .reshape(sum_shape[:2] + (2 * STATE,))
     )
     s3 = sum_start(r["p2"], r["q2"])
+    lax.fori_loop(0, groups, gather_sums, 0)
     t1 = [net.go(sg_ref.at[net.z_of(k)], r["sr"].at[k], net.at_z(k)) for k in range(1, nz)]
     sa_ref, sb_ref, rra_ref, rrb_ref = r["sa"], r["sb"], r["rra"], r["rrb"]
-    lo, hi = pl.ds(0, half_width), pl.ds(half_width, half_width)
 
     def add_a(i, carry):
-        total = dw_ref[z, i, :, lo].astype(F32)
-        for k in range(1, nz):
-            total = total + ra_ref[k, i, :, lo].astype(F32)
-        sa_ref[i] = total.astype(BF16)
+        for p in range(pairs):
+            at, to = pl.ds(2 * p * LANES, LANES), pl.ds(p * LANES, LANES)
+            total = dw_ref[z, i, :, at].astype(F32)
+            for k in range(1, nz):
+                total = total + ra_ref[k, i, :, at].astype(F32)
+            sa_ref[i, :, to] = total.astype(BF16)
         return carry
 
     def add_b(i, carry):
-        total = dw_ref[i, y, :, hi].astype(F32)
-        for k in range(1, ny):
-            total = total + ra_ref[k, i, :, hi].astype(F32)
-        sb_ref[i] = total.astype(BF16)
+        for p in range(pairs):
+            at, to = pl.ds((2 * p + 1) * LANES, LANES), pl.ds(p * LANES, LANES)
+            total = dw_ref[i, y, :, at].astype(F32)
+            for k in range(1, ny):
+                total = total + ra_ref[k, i, :, at].astype(F32)
+            sb_ref[i, :, to] = total.astype(BF16)
         return carry
 
     s4 = sum_turn(s3, r["p2"], r["q2"], r["acc2"], r["gproj"])
-    arrived([dw_copy(p, k, True) for p in range(pairs // 2) for k in range(1, nz)])
+    arrived([dw_copy(p, k, True) for p in range(pairs) for k in range(1, nz)])
     lax.fori_loop(0, ny, add_a, 0)
     a2nd = [net.go(sa_ref.at[net.y_of(k)], rra_ref.at[k], net.at_y(k)) for k in range(1, ny)]
-    arrived([dw_copy(p, k, False) for p in range(pairs // 2, pairs) for k in range(1, ny)])
+    arrived([dw_copy(p, k, False) for p in range(pairs) for k in range(1, ny)])
     lax.fori_loop(0, nz, add_b, 0)
     b2nd = [net.go(sb_ref.at[net.z_of(k)], rrb_ref.at[k], net.at_z(k)) for k in range(1, nz)]
     arrived(t1)
@@ -642,6 +696,9 @@
 
     out_ref, head_ref, cg_ref = r["grad"], r["head"], r["cg"]
     out_ref[...] = dot(r["gproj"][...].reshape(tokens, PROJ), wo_ref[...].reshape(width, PROJ), ((1,), (1,)))
+
+    rows_ref = r["rows"]
+    rows_ref[...] = jnp.zeros(rows_ref.shape, F32)
 
     def close(g, carry):
         at = lanes_of(g)
@@ -655,9 +712,9 @@
         padded = with_earlier(x, edge, CONV - 1)
         for k in range(CONV):
             part = jnp.sum(grad * padded[k : k + x.shape[0]], axis=0)
-            cg_ref[g, pl.ds(k, 1)] = jnp.sum(part, axis=0, keepdims=True)
-        cg_ref[g, pl.ds(CONV, 1)] = jnp.sum(jnp.sum(grad, axis=0), axis=0, keepdims=True)
-        cg_ref[g, pl.ds(CONV + 1, 3)] = jnp.zeros((3, LANES), F32)
+            rows_ref[pl.ds(k, 1)] = jnp.sum(part, axis=0, keepdims=True)
+        rows_ref[pl.ds(CONV, 1)] = jnp.sum(jnp.sum(grad, axis=0), axis=0, keepdims=True)
+        cg_ref[g] = rows_ref[...].astype(BF16)
         head_ref[:, at] = jnp.zeros((CHUNKS, LANES), F32)
         for k in range(CONV - 1):
             head_ref[pl.ds(k, 1), at] = grad[k, 0:1]
@@ -670,22 +727,24 @@
     total = sa_ref[y].astype(F32)
     for k in range(1, ny):
         total = total + rra_ref[k].astype(F32)
-    r["dwo"][:, lo] = total
+    for p in range(pairs):
+        r["dwo"][:, pl.ds(2 * p * LANES, LANES)] = total[:, p * LANES : (p + 1) * LANES]
     arrived(b2nd)
     total = sb_ref[z].astype(F32)
     for k in range(1, nz):
         total = total + rrb_ref[k].astype(F32)
-    r["dwo"][:, hi] = total
+    for p in range(pairs):
+        r["dwo"][:, pl.ds((2 * p + 1) * LANES, LANES)] = total[:, p * LANES : (p + 1) * LANES]
     arrived(t2)
     total = r["ss"][...]
     for k in range(1, ny):
         total = total + r["srr"][k]
     r["smallo"][pl.ds(CHUNKS, 24)] = total
     arrived(u1)
-    total = cg_ref[z]
+    total = cg_ref[z].astype(F32)
     for k in range(1, nz):
-        total = total + r["cr"][k]
-    r["cs"][...] = total
+        total = total + r["cr"][k].astype(F32)
+    r["cs"][...] = total.astype(BF16)
     u2 = [net.go(r["cs"], r["crr"].at[k], net.at_y(k)) for k in range(1, ny)]
     later.wait_recv()
     last_block = net.me == n_ctx - 1
@@ -710,13 +769,14 @@
         pack_copy(k).wait_send()
         edge_copy(k).wait_send()
     for p in range(pairs):
-        along_z = p < pairs // 2
-        for k in range(1, nz if along_z else ny):
-            dw_copy(p, k, along_z).wait_send()
+        for k in range(1, nz):
+            dw_copy(p, k, True).wait_send()
+        for k in range(1, ny):
+            dw_copy(p, k, False).wait_send()
     arrived(u2)
-    total = r["cs"][...]
+    total = r["cs"][...].astype(F32)
     for k in range(1, ny):
-        total = total + r["crr"][k]
+        total = total + r["crr"][k].astype(F32)
     r["smallo"][pl.ds(0, CHUNKS)] = total
     net.finish()
 
@@ -849,11 +909,20 @@
         later=((CHUNKS, width), F32),
         grad=(full, F32),
         flow=((tokens, LANES), F32),
+        low_sum=((tokens, RANK), F32),
+        run=((STATE, CHUNKS, width), F32),
+        wl=((STATE, CHUNKS, width), F32),
+        wr=((STATE, CHUNKS, width), F32),
+        total=((CHUNKS, width), F32),
+        rs=((groups, STATE, CHUNKS, LANES), F32),
+        ps=((groups, 2, CHUNKS, LANES), F32),
+        decay=((groups,) + wide, F32),
         slope=((tokens, LANES), F32),
-        cg=((groups, CHUNKS, LANES), F32),
-        cr=((nz, CHUNKS, LANES), F32),
-        cs=((CHUNKS, LANES), F32),
-        crr=((ny, CHUNKS, LANES), F32),
+        rows=((CHUNKS, LANES), F32),
+        cg=((groups, CHUNKS, LANES), BF16),
+        cr=((nz, CHUNKS, LANES), BF16),
+        cs=((CHUNKS, LANES), BF16),
+        crr=((ny, CHUNKS, LANES), BF16),
     )
     names = list(inputs) + list(outs) + list(scratch) + ["send", "recv"]
     slots = 256

time: 98.4 us -> 97.6 us (level)
  no operation moved by 1% of the time
where the time goes in v4:
time: 97.6 us; the launch traced here: 96.6 us
  Pallas kernels  95.9 us (98%)
    pallas_call x2, Pallas kernels, call(): pl.pallas_call(kernel, out_shape=tuple((jax.ShapeDtypeStruct(s, d) for s,...  95.9 us

profile of v4, /device:TPU:6, one launch (start us, length us, event | category | flops | bytes accessed | tf_op | source)
XLA Modules:
  0.0 96.6 jit_solution(11998162940585523782)
XLA Ops:
  0.6 93.9 %shard_map.170 = (bf16[128,1024]{1,0:T(8,128)(2,1)}, bf16[128,1024]{1,0:T(8,128)(2,1)}, f32[8,1024]{1,0:T(8,128)}, f32[32,128]{1,0:T(8,128)}) custom-call(bf16[128,1024]{1,0:T(8,128)(2,1)} %refs_0_.1, bf16[128,1024]{1,0:T(8,128)(2,1)} %refs_1_.1, bf16[128,1024]{1,0:T(8,128)(2,1)} %refs_2_.1, s32[1,128]{1,0:T(1,128)} %bitcast.10, f32[4,1024]{1,0:T(4,128)} %refs_4_.1, ...), custom_call_target="tpu_custom_call" | custom-call | tf_op jit(solution)/shard_map/pallas_call | solution.py:36
  94.5 2.1 %shard_map.171 = (bf16[128,1024]{1,0:T(8,128)(2,1)}, bf16[128,1024]{1,0:T(8,128)(2,1)}, f32[8,1024]{1,0:T(8,128)}, f32[4,16]{1,0:T(4,128)}, f32[1,16]{1,0:T(1,12...) custom-call(bf16[128,1024]{1,0:T(8,128)(2,1)} %get-tuple-element.20.seq_ref, ...), custom_call_target="tpu_custom_call" | custom-call | tf_op jit(solution)/shard_map/pallas_call | solution.py:36
